TPU v7x, 256 devices: a whole 4x4x8 slice. The times are simulated.
256 devices in a mesh: sect: 4 (over x_lo, core), slab: 64 (over x_hi, y, z).
Axes of the slice: x: 4 (x_hi: 2, x_lo: 2; x = x_hi * 2 + x_lo), y: 4, z: 8, core: 2. Of those that a mesh axis runs over, the one named last changes fastest.
Arguments:
- density: float32 [512, 128, 128], P('slab', 'sect'), may hold values from 0.3 to 3
- velocity: float32 [3, 512, 128, 128], P(None, 'slab', 'sect'), may hold values from -4.8 to 4.8, as said below
- pressure: float32 [512, 128, 128], P('slab', 'sect'), may hold values from 0.3 to 3
- owners: int32 [128, 4, 1], P('sect'), may hold values from 0 to 63; in each aligned block of 128 rows (0 to 127, 128 to 255, ..., all dimensions but the last counted through in order) at most 4 rows name the same one
Outputs:
- new_state: float32 [5, 512, 128, 128], P(None, 'slab', 'sect')
- optical_depth: float32 [4, 64, 4, 512], P('sect', 'slab')
Inputs may be any that keep to these rules, and one draw needn't show every extreme that they name: velocity components are real values within the range. `owners`: among the sightlines of one section (the aligned block of 128 rows) no index is named more than 4 times, a bound that some block reaches.
All inputs are finite; a program needn't handle non-finite values. Where the computation divides by a largest or mean magnitude, that divisor is 1e-20 or more.
Results may differ from a plain program's by a relative error of at most 0.0001.
Values sent between devices are 32-bit elements; how exact they have to be, the bound alone decides.
A program may use at most 128 MiB of HBM per device.

v0:
```python
import jax
import jax.numpy as jnp
from jax import lax
from jax.sharding import Mesh
from jax.sharding import PartitionSpec as P

STRIDE = 32
BAND = 512
SECT_SLAB = ("sect_0", "sect_1", "slab_0", "slab_1", "slab_2")
SECT = ("sect_0", "sect_1")
SLAB = ("slab_0", "slab_1", "slab_2")


GAMMA = 5.0 / 3.0
COURANT = 0.15
TURBULENT = 0.25
NORMALISE = 0.5641895835477563


def over_axes(x, axes):
    for axis in axes:
        x = lax.pmax(x, axis)
    return x


def padded_2(x, sides, width):
    edges = {}
    for axis, dim in sides:
        size, length = (lax.axis_size(axis), x.shape[dim])
        up = [(i, (i + 1) % size) for i in range(size)]
        last = lax.slice_in_dim(x, length - width, length, axis=dim)
        leading = lax.slice_in_dim(x, 0, width, axis=dim)
        edges[dim] = (
            lax.ppermute(last, axis, up),
            lax.ppermute(leading, axis, [(b, a) for a, b in up]),
        )
    done = []
    for _, dim in sides:
        low, high = edges[dim]
        around = [(width, width) if d in done else (0, 0) for d in range(x.ndim)]
        x = jnp.concatenate([jnp.pad(low, around), x, jnp.pad(high, around)], axis=dim)
        done.append(dim)
    return x


def primitives(current):
    density = current[0]
    velocity = current[1:4] / density
    pressure = (GAMMA - 1.0) * (current[4] - 0.5 * jnp.sum(current[1:4] * velocity, axis=0))
    return (density, velocity, pressure)


def conserved(density, velocity, pressure):
    momentum = density[None] * velocity
    energy = pressure / (GAMMA - 1.0) + 0.5 * jnp.sum(momentum * velocity, axis=0)
    return jnp.concatenate([density[None], momentum, energy[None]], axis=0)


def physical_flux(current, velocity, pressure, axis_dim):
    moving = velocity[axis_dim]
    pieces = [current[axis_dim + 1]]
    for component in range(3):
        summand = current[component + 1] * moving
        if component == axis_dim:
            summand = summand + pressure
        pieces.append(summand)
    pieces.append((current[4] + pressure) * moving)
    return jnp.stack(pieces, axis=0)


def face_flux(left_state, right_state, axis_dim):
    left_density, left_velocity, left_pressure = primitives(left_state)
    right_density, right_velocity, right_pressure = primitives(right_state)
    left_speed = jnp.abs(left_velocity[axis_dim]) + jnp.sqrt(GAMMA * left_pressure / left_density)
    right_speed = jnp.abs(right_velocity[axis_dim]) + jnp.sqrt(
        GAMMA * right_pressure / right_density
    )
    signal_speed = jnp.maximum(left_speed, right_speed)
    average = 0.5 * (
        physical_flux(left_state, left_velocity, left_pressure, axis_dim)
        + physical_flux(right_state, right_velocity, right_pressure, axis_dim)
    )
    return average - 0.5 * signal_speed[None] * (right_state - left_state)


def line_inputs(current):
    density, velocity, pressure = primitives(current)
    broadening = TURBULENT + pressure / density
    return jnp.stack([density, broadening, velocity[0]], axis=0)


def line_params(fields):
    width = BAND / 64.0 * jnp.sqrt(fields[1])
    amplitude = NORMALISE * jnp.square(fields[0]) * jnp.power(fields[1], -0.7) / width
    return jnp.stack([amplitude, 1.0 / width, BAND / 8.0 * fields[2]], axis=0)


def skewer_depth(params):
    length = params.shape[2]
    half_band = BAND // 2
    offsets = (jnp.arange(BAND, dtype=jnp.int32) - half_band).astype(jnp.float32)[:, None]
    repeats = (length + BAND) // length + 2
    first_col = -half_band % length

    def one_line(line_parts):
        amplitude, inverse, line_shift = line_parts
        summands = amplitude[None, :] * jnp.exp(
            -jnp.square((offsets - line_shift[None, :]) * inverse[None, :])
        )
        tiled = jnp.tile(summands, (1, repeats))[:, first_col : first_col + length + BAND]
        flattened = tiled.reshape(-1)[BAND : BAND + BAND * (length + BAND - 1)]
        return jnp.sum(flattened.reshape(BAND, length + BAND - 1)[:, :length], axis=0)

    return lax.map(one_line, (params[0], params[1], params[2]))


def depth_lines(arrived):
    return skewer_depth(arrived)


def body(density, velocity, pressure, owners):
    current = conserved(density, velocity, pressure)
    sound_speed = jnp.sqrt(GAMMA * pressure / density)
    fastest = over_axes(jnp.max(jnp.abs(velocity) + sound_speed[None]), SECT_SLAB)
    time_step = COURANT / fastest
    padded = padded_2(current, ((SECT, 2), (SLAB, 1)), 1)
    inner_rows = padded[:, :, 1:-1, :]
    first_flux = face_flux(inner_rows[:, :-1], inner_rows[:, 1:], 0)
    change = first_flux[:, 1:] - first_flux[:, :-1]
    middle = padded[:, 1:-1]
    second_flux = face_flux(middle[:, :, :-1], middle[:, :, 1:], 1)
    change = change + (second_flux[:, :, 1:] - second_flux[:, :, :-1])
    third_flux = face_flux(current, jnp.roll(current, -1, axis=3), 2)
    change = change + (third_flux - jnp.roll(third_flux, 1, axis=3))
    new_state = current - time_step * change
    sampled = line_inputs(new_state[:, :, :, ::STRIDE])
    fields = line_params(sampled)
    width_x = fields.shape[1]
    columns = fields.shape[2] * fields.shape[3]
    by_column = jnp.transpose(fields.reshape(3, width_x, columns), (0, 2, 1))
    group_size = lax.axis_size(SLAB)
    most_slots = 2 * columns // group_size
    owner_flat = owners.reshape(columns)
    choose = (owner_flat[:, None] == jnp.arange(group_size, dtype=jnp.int32)[None, :]).astype(
        jnp.int32
    )
    ranking = jnp.sum((jnp.cumsum(choose, axis=0) - choose) * choose, axis=1)
    per_device = columns // group_size
    arrived = lax.all_to_all(by_column, SLAB, split_axis=1, concat_axis=2, tiled=True)
    local_depth = depth_lines(arrived)
    my_index = lax.axis_index(SLAB)
    block_owner = lax.dynamic_slice_in_dim(owner_flat, my_index * per_device, per_device)
    keep_mask = block_owner[None, :] == jnp.arange(group_size, dtype=jnp.int32)[:, None]
    outgoing = jnp.where(keep_mask[:, :, None], local_depth[None], 0.0).reshape(
        group_size * per_device, local_depth.shape[1]
    )
    returned = lax.all_to_all(outgoing, SLAB, split_axis=0, concat_axis=0, tiled=True)
    target = jnp.where(owner_flat == my_index, ranking, most_slots)
    source_rows = jnp.full((most_slots,), columns, jnp.int32)
    source_rows = source_rows.at[target].set(jnp.arange(columns, dtype=jnp.int32), mode="drop")
    padded_back = jnp.concatenate(
        [returned, jnp.zeros((1, returned.shape[1]), jnp.float32)], axis=0
    )
    depth_rows = jnp.take(padded_back, source_rows, axis=0)
    return (new_state, depth_rows.reshape(1, 1, most_slots, depth_rows.shape[1]))


def solution(mesh):
    split = Mesh(
        mesh.devices.reshape(2, 2, 2, 4, 8), ("sect_0", "sect_1", "slab_0", "slab_1", "slab_2")
    )
    placed = (
        P(SLAB, SECT, None),
        P(None, SLAB, SECT, None),
        P(SLAB, SECT, None),
        P(SECT, None, None),
    )
    return jax.shard_map(
        body,
        mesh=split,
        in_specs=placed,
        out_specs=(P(None, SLAB, SECT, None), P(SECT, SLAB, None, None)),
        check_vma=False,
    )
```

profile of v0, /device:TPU:32, one launch (start us, length us, event | category | flops | bytes accessed | tf_op | source)
XLA Modules:
  0.0 216.3 jit_solution(7761970011789050115)
XLA Ops:
  12.0 3.0 %copy.152 = f32[5,8,32,128]{2,1,3,0:T(8,128)} copy(f32[5,8,32,128]{3,2,1,0:T(8,128)} %pad_maximum_fusion.1) | data formatting | bytes 1310720 | tf_op jit(solution)/shard_map/jit(_roll_static)/concatenate | solution.py:133
  23.0 5.5 %pmax.35 = f32[]{:T(128)} all-reduce(f32[]{:T(128)} %get-tuple-element.59), channel_id=1, replica_groups=mesh['sect_0'=2,'sect_1'=2,'slab_0'=2,'slab_1'=4,'slab_2'=8] {'sect_0'}, use_global_device_ids=true, to_apply=%region_2.0 | all-reduce | flops 1 | bytes 8 | tf_op jit(solution)/shard_map/pmax | solution.py:22
  28.6 3.0 %copy.149 = f32[5,8,32,128]{2,1,3,0:T(8,128)} copy(f32[5,8,32,128]{3,2,1,0:T(8,128)} %bitcast_dynamic-update-slice_fusion) | data formatting | bytes 1310720 | tf_op jit(solution)/shard_map/stack | solution.py:68
  31.6 3.1 %pmax.36 = f32[]{:T(128)} all-reduce(f32[]{:T(128)} %pmax.35), channel_id=1, replica_groups=mesh['sect_0'=2,'sect_1'=2,'slab_0'=2,'slab_1'=4,'slab_2'=8] {'sect_1'}, use_global_device_ids=true, to_apply=%region_3.0 | all-reduce | flops 1 | bytes 8 | tf_op jit(solution)/shard_map/pmax | solution.py:22
  36.9 7.0 %pmax.37 = f32[]{:T(128)} all-reduce(f32[]{:T(128)} %pmax.36), channel_id=1, replica_groups=mesh['sect_0'=2,'sect_1'=2,'slab_0'=2,'slab_1'=4,'slab_2'=8] {'slab_0'}, use_global_device_ids=true, to_apply=%region_4.0 | all-reduce | flops 1 | bytes 8 | tf_op jit(solution)/shard_map/pmax | solution.py:22
  44.2 11.4 %pmax.38 = f32[]{:T(128)} all-reduce(f32[]{:T(128)} %pmax.37), channel_id=1, replica_groups=mesh['sect_0'=2,'sect_1'=2,'slab_0'=2,'slab_1'=4,'slab_2'=8] {'slab_1'}, use_global_device_ids=true, to_apply=%region_5.0 | all-reduce | flops 1 | bytes 8 | tf_op jit(solution)/shard_map/pmax | solution.py:22
  56.2 5.4 %multiply_subtract_fusion.1 = f32[5,8,32,128]{2,1,3,0:T(8,128)} fusion(f32[5,8,32,128]{2,1,3,0:T(8,128)} %copy.152, f32[5,8,32,128]{2,1,3,0:T(8,128)S(1)} %copy.154, f32[5,8,32,128]{2,1,3,0:T(8,128)} %copy.149, f32[5,8,32,128]{2,1,3,0:T(8,128)} %copy.150, f32[8,32,128]{1,0,2:T(8,128)S(1)} %copy.151), kind=kLoop, calls=%fused_computation.21 | loop fusion | flops 819200 | bytes 3407872 | tf_op jit(solution)/shard_map/sub | solution.py:83
  61.7 20.5 %pmax.39 = f32[]{:T(128)} all-reduce(f32[]{:T(128)} %pmax.38), channel_id=1, replica_groups=mesh['sect_0'=2,'sect_1'=2,'slab_0'=2,'slab_1'=4,'slab_2'=8] {'slab_2'}, use_global_device_ids=true, to_apply=%region_6.0 | all-reduce | flops 1 | bytes 8 | tf_op jit(solution)/shard_map/pmax | solution.py:22
  82.2 3.4 %slice.386 = f32[5,8,32,127]{2,1,3,0:T(8,128)} slice(f32[5,8,32,128]{2,1,3,0:T(8,128)} %multiply_subtract_fusion.1), slice={[0:5], [0:8], [0:32], [0:127]} | slice | bytes 1300480 | tf_op jit(solution)/shard_map/jit(_roll_static)/slice | solution.py:134
  87.1 3.0 %copy.148 = f32[5,8,1,128]{2,1,3,0:T(8,128)} copy(f32[5,8,1,128]{3,1,2,0:T(8,128)} %collective-permute-done.2) | data formatting | bytes 40960 | tf_op jit(solution)/shard_map/ppermute | solution.py:35
  90.1 3.0 %copy.145 = f32[5,8,1,128]{2,1,3,0:T(8,128)} copy(f32[5,8,1,128]{3,1,2,0:T(8,128)} %collective-permute-done.1) | data formatting | bytes 40960 | tf_op jit(solution)/shard_map/ppermute | solution.py:34
  102.3 5.0 %fusion.7 = f32[5,8,33,128]{2,1,3,0:T(8,128)} fusion(f32[5,8,33,128]{2,1,3,0:T(8,128)S(1)} %get-tuple-element.85, f32[5,8,33,128]{2,1,3,0:T(8,128)} %copy-done.9, f32[5,8,32,128]{2,1,3,0:T(8,128)S(1)} %copy.154, f32[5,8,1,128]{2,1,3,0:T(8,128)S(1)} %copy-done.1, f32[5,8,1,128]{2,1,3,0:T(8,128)S(1)} %copy-done, f32[8,33,128]{1,0,2:T(8,128)S(1)} %get-tuple-element.84), kind=kLoop, calls=%fused_computation.19 | loop fusion | flops 1182720 | bytes 2859008 | tf_op jit(solution)/shard_map/sub | solution.py:83
  112.2 4.8 %copy.143 = f32[5,9,32,128]{2,1,3,0:T(8,128)} copy(f32[5,9,32,128]{3,2,1,0:T(8,128)} %slice.334) | data formatting | bytes 1474560 | tf_op jit(solution)/shard_map/slice | solution.py:128
  117.0 4.8 %copy.144 = f32[5,9,32,128]{2,1,3,0:T(8,128)} copy(f32[5,9,32,128]{3,2,1,0:T(8,128)} %slice.335) | data formatting | bytes 1474560 | tf_op jit(solution)/shard_map/slice | solution.py:128
  127.3 4.8 %copy.140 = f32[5,9,32,128]{2,1,3,0:T(8,128)} copy(f32[5,9,32,128]{3,2,1,0:T(8,128)} %get-tuple-element.98) | data formatting | bytes 1474560 | tf_op jit(solution)/shard_map/stack | solution.py:68
  132.2 3.9 %copy.141 = f32[5,9,32,128]{2,1,3,0:T(8,128)} copy(f32[5,9,32,128]{3,2,1,0:T(8,128)S(1)} %copy-done.20) | data formatting | bytes 1474560 | tf_op jit(solution)/shard_map/stack | solution.py:68
  137.5 11.0 %multiply_subtract_fusion = f32[5,9,32,128]{2,1,3,0:T(8,128)} fusion(f32[5,9,32,128]{2,1,3,0:T(8,128)} %copy.143, f32[5,9,32,128]{2,1,3,0:T(8,128)} %copy.144, f32[5,9,32,128]{2,1,3,0:T(8,128)} %copy.140, f32[5,9,32,128]{2,1,3,0:T(8,128)} %copy.141, f32[9,32,128]{1,0,2:T(8,128)} %copy.142), kind=kLoop, calls=%fused_computation.10 | loop fusion | flops 921600 | bytes 3833856 | tf_op jit(solution)/shard_map/sub | solution.py:83
  148.5 7.2 %fusion.5 = f32[5,8,32,128]{2,1,3,0:T(8,128)S(1)} fusion(f32[5,8,32,128]{2,1,3,0:T(8,128)S(1)} %copy.154, f32[5,8,33,128]{2,1,3,0:T(8,128)} %fusion.7, f32[5,9,32,128]{2,1,3,0:T(8,128)} %multiply_subtract_fusion, f32[5,8,32,128]{2,1,3,0:T(8,128)} %multiply_subtract_fusion.1, f32[5,8,32,127]{2,1,3,0:T(8,128)} %slice.386, f32[5,8,32,1]{2,1,3,0:T(8,128)S(1)} %slice-done, ...), kind=kLoop, calls=%fused_computation.15 | loop fusion | flops 1310720 | bytes 5242884 | tf_op jit(solution)/shard_map/sub | solution.py:135
  158.4 7.8 %all-to-all-start = ((f32[3,128,8]{2,0,1:T(4,128)}), f32[3,128,8]{2,0,1:T(4,128)S(1)}, u32[]{:S(2)}, u32[]{:S(2)}) async-start(f32[3,128,8]{2,0,1:T(4,128)} %copy.160), calls=%async_computation | async-start | bytes 524288 | tf_op jit(solution)/shard_map/all_to_all | solution.py:149
  167.2 12.2 %all-to-all-done = f32[3,128,8]{2,0,1:T(4,128)S(1)} async-done(((f32[3,128,8]{2,0,1:T(4,128)}), f32[3,128,8]{2,0,1:T(4,128)S(1)}, u32[]{:S(2)}, u32[]{:S(2)}) %all-to-all-start) | async-done | bytes 12320 | tf_op jit(solution)/shard_map/all_to_all | solution.py:149
  179.8 15.9 %while.11 = (s32[]{:T(128)}, f32[2,512]{1,0:T(2,128)S(1)}, f32[2,512]{1,0:T(2,128)S(1)}, f32[2,512]{1,0:T(2,128)S(1)}, f32[2,512]{1,0:T(2,128)S(1)}, /*index=5*/s32[]{:T(128)}, s32[]{:T(128)}) while((s32[]{:T(128)}, f32[2,512]{1,0:T(2,128)S(1)}, f32[2,512]{1,0:T(2,128)S(1)}, f32[2,512]{1,0:T(2,128)S(1)}, ...), condition=%wide.region_19.20_spmd.clone, body=%wide.region_17.19_spmd.clone.sunk | while | flops 1573378 | bytes 32526432 | solution.py:114
  196.6 5.0 %all-to-all-start.1 = ((f32[64,2,512]{2,1,0:T(2,128)}), f32[64,2,512]{2,1,0:T(2,128)S(1)}, u32[]{:S(2)}, u32[]{:S(2)}) async-start(f32[64,2,512]{2,1,0:T(2,128)} %broadcast_select_fusion), calls=%async_computation.1 | async-start | bytes 524288 | tf_op jit(solution)/shard_map/all_to_all | solution.py:157
  201.6 3.0 %copy.165 = f32[5,8,32,128]{3,2,1,0:T(8,128)} copy(f32[5,8,32,128]{2,1,3,0:T(8,128)} %copy-done.6) | data formatting | bytes 1310720
  204.6 10.2 %all-to-all-done.1 = f32[64,2,512]{2,1,0:T(2,128)S(1)} async-done(((f32[64,2,512]{2,1,0:T(2,128)}), f32[64,2,512]{2,1,0:T(2,128)S(1)}, u32[]{:S(2)}, u32[]{:S(2)}) %all-to-all-start.1) | async-done | bytes 262176 | tf_op jit(solution)/shard_map/all_to_all | solution.py:157
  (173 shorter events, 66.2 us)
Async XLA Ops:
  3.5 4.7 %copy-start.7 = (f32[3,8,32,128]{3,2,1,0:T(8,128)}, f32[3,8,32,128]{3,2,1,0:T(8,128)S(1)}, u32[]{:S(2)}) copy-start(f32[3,8,32,128]{3,2,1,0:T(8,128)S(1)} %get-tuple-element.112) | copy-start | bytes 1179652
  3.5 4.7 %copy-start.14 = (f32[3,8,32,128]{3,2,1,0:T(8,128)}, f32[3,8,32,128]{3,2,1,0:T(8,128)S(1)}, u32[]{:S(2)}) copy-start(f32[3,8,32,128]{3,2,1,0:T(8,128)S(1)} %get-tuple-element.113) | copy-start | bytes 1179652
  3.5 4.7 %copy-start.15 = (f32[8,32,128]{2,1,0:T(8,128)}, f32[8,32,128]{2,1,0:T(8,128)S(1)}, u32[]{:S(2)}) copy-start(f32[8,32,128]{2,1,0:T(8,128)S(1)} %get-tuple-element.57) | copy-start | bytes 393220
  3.7 4.6 %copy-start.22 = (f32[5,8,32,128]{3,2,1,0:T(8,128)}, f32[5,8,32,128]{3,2,1,0:T(8,128)S(1)}, u32[]{:S(2)}) copy-start(f32[5,8,32,128]{3,2,1,0:T(8,128)S(1)} %get-tuple-element.74) | copy-start | bytes 1966084
  3.7 16.1 %copy-start.12 = (f32[8,32,128]{2,1,0:T(8,128)}, f32[8,32,128]{2,1,0:T(8,128)S(1)}, u32[]{:S(2)}) copy-start(f32[8,32,128]{2,1,0:T(8,128)S(1)} %get-tuple-element.75) | copy-start | bytes 393220
  4.7 82.4 %collective-permute-start.2 = (f32[5,8,1,128]{3,1,2,0:T(8,128)}, f32[5,8,1,128]{3,1,2,0:T(8,128)}, u32[]{:S(2)}, u32[]{:S(2)}) collective-permute-start(f32[5,8,1,128]{3,1,2,0:T(8,128)} %bitcast.40), channel_id=1, source_target_pairs={{64,0},{128,64},{192,128},{0,192},{65,1},{129,65},{193,129},{1,193... | collective-permute-start | bytes 61448 | tf_op jit(solution)/shard_map/ppermute | solution.py:35
  5.6 84.5 %collective-permute-start.1 = (f32[5,8,1,128]{3,1,2,0:T(8,128)}, f32[5,8,1,128]{3,1,2,0:T(8,128)}, u32[]{:S(2)}, u32[]{:S(2)}) collective-permute-start(f32[5,8,1,128]{3,1,2,0:T(8,128)} %bitcast.39), channel_id=1, source_target_pairs={{0,64},{64,128},{128,192},{192,0},{1,65},{65,129},{129,193},{193,1... | collective-permute-start | bytes 61448 | tf_op jit(solution)/shard_map/ppermute | solution.py:34
  6.3 101.0 %collective-permute-start = (f32[5,1,32,128]{3,2,1,0:T(8,128)}, f32[5,1,32,128]{3,2,1,0:T(8,128)}, u32[]{:S(2)}, u32[]{:S(2)}) collective-permute-start(f32[5,1,32,128]{3,2,1,0:T(8,128)} %get-tuple-element.108), channel_id=1, source_target_pairs={{0,1},{1,2},{2,3},{3,4},{4,5},{5,6},{6,7},{7,8},{8,9},{9,10},{10,1... | collective-permute-start | bytes 245768 | tf_op jit(solution)/shard_map/ppermute | solution.py:34
  8.2 99.1 %collective-permute-start.3 = (f32[5,1,32,128]{3,2,1,0:T(8,128)}, f32[5,1,32,128]{3,2,1,0:T(8,128)}, u32[]{:S(2)}, u32[]{:S(2)}) collective-permute-start(f32[5,1,32,128]{3,2,1,0:T(8,128)} %get-tuple-element.109), channel_id=1, source_target_pairs={{1,0},{2,1},{3,2},{4,3},{5,4},{6,5},{7,6},{8,7},{9,8},{10,9},{11,1... | collective-permute-start | bytes 245768 | tf_op jit(solution)/shard_map/ppermute | solution.py:35
  15.0 3.2 %copy-start.3 = (f32[5,8,32,127]{3,2,1,0:T(8,128)S(1)}, f32[5,8,32,127]{3,2,1,0:T(8,128)}, u32[]{:S(2)}) copy-start(f32[5,8,32,127]{3,2,1,0:T(8,128)} %copy-done.2) | copy-start | bytes 1950724
  23.0 11.7 %copy-start.21 = (f32[5,8,32,128]{3,2,1,0:T(8,128)S(1)}, f32[5,8,32,128]{3,2,1,0:T(8,128)}, u32[]{:S(2)}) copy-start(f32[5,8,32,128]{3,2,1,0:T(8,128)} %multiply_dynamic-update-slice_fusion.4) | copy-start | bytes 1966084
  28.6 15.4 %copy-start.25 = (f32[8,32,128]{2,1,0:T(8,128)S(1)}, f32[8,32,128]{2,1,0:T(8,128)}, u32[]{:S(2)}) copy-start(f32[8,32,128]{2,1,0:T(8,128)} %fusion.50) | copy-start | bytes 393220
  31.6 24.0 %copy-start.26 = (s32[32,4,1]{0,2,1:T(1,128)S(1)}, s32[32,4,1]{0,2,1:T(1,128)}, u32[]{:S(2)}) copy-start(s32[32,4,1]{0,2,1:T(1,128)} %param.9) | copy-start | bytes 1540
  102.3 5.0 %copy-start.8 = (f32[3,8,32,128]{3,2,1,0:T(8,128)S(1)}, f32[3,8,32,128]{3,2,1,0:T(8,128)}, u32[]{:S(2)}) copy-start(f32[3,8,32,128]{3,2,1,0:T(8,128)} %copy-done.7) | copy-start | bytes 1179652
  102.3 5.0 %copy-start.11 = (f32[8,32,128]{2,1,0:T(8,128)S(1)}, f32[8,32,128]{2,1,0:T(8,128)}, u32[]{:S(2)}) copy-start(f32[8,32,128]{2,1,0:T(8,128)} %param.6) | copy-start | bytes 393220
  102.3 5.0 %copy-start.13 = (f32[8,32,128]{2,1,0:T(8,128)S(1)}, f32[8,32,128]{2,1,0:T(8,128)}, u32[]{:S(2)}) copy-start(f32[8,32,128]{2,1,0:T(8,128)} %copy-done.12) | copy-start | bytes 393220
  121.8 3.6 %copy-start.5 = (f32[5,9,34,128]{3,2,1,0:T(8,128)S(1)}, f32[5,9,34,128]{3,2,1,0:T(8,128)}, u32[]{:S(2)}) copy-start(f32[5,9,34,128]{3,2,1,0:T(8,128)} %copy-done.4) | copy-start | bytes 2350084
  121.8 3.6 %copy-start.18 = (f32[5,9,32,128]{3,2,1,0:T(8,128)S(1)}, f32[5,9,32,128]{3,2,1,0:T(8,128)}, u32[]{:S(2)}) copy-start(f32[5,9,32,128]{3,2,1,0:T(8,128)} %get-tuple-element.103) | copy-start | bytes 2211844
  127.3 4.9 %copy-start.20 = (f32[5,9,32,128]{3,2,1,0:T(8,128)S(1)}, f32[5,9,32,128]{3,2,1,0:T(8,128)}, u32[]{:S(2)}) copy-start(f32[5,9,32,128]{3,2,1,0:T(8,128)} %copy-done.19) | copy-start | bytes 2211844
  132.1 3.9 %copy-start.23 = (f32[9,32,128]{2,1,0:T(8,128)S(1)}, f32[9,32,128]{2,1,0:T(8,128)}, u32[]{:S(2)}) copy-start(f32[9,32,128]{2,1,0:T(8,128)} %get-tuple-element.97) | copy-start | bytes 442372
  137.5 11.0 %slice-start = ((f32[5,8,32,128]{2,1,3,0:T(8,128)}), f32[5,8,32,1]{2,1,3,0:T(8,128)S(1)}, s32[]{:S(2)}) async-start(f32[5,8,32,128]{2,1,3,0:T(8,128)} %multiply_subtract_fusion.1), calls=%async_computation.2 | async-start | bytes 40960 | tf_op jit(solution)/shard_map/jit(_roll_static)/slice | solution.py:134
  148.5 17.7 %copy-start.27 = (pred[128,1]{0,1:T(4,128)(4,1)S(1)}, pred[128,1]{0,1:T(4,128)(4,1)}, u32[]{:S(2)}) copy-start(pred[128,1]{0,1:T(4,128)(4,1)} %eq.50) | copy-start | bytes 388
  158.4 21.1 %all-to-all-start = ((f32[3,128,8]{2,0,1:T(4,128)}), f32[3,128,8]{2,0,1:T(4,128)S(1)}, u32[]{:S(2)}, u32[]{:S(2)}) async-start(f32[3,128,8]{2,0,1:T(4,128)} %copy.160), calls=%async_computation | async-start | bytes 524288 | tf_op jit(solution)/shard_map/all_to_all | solution.py:149
  196.6 18.3 %all-to-all-start.1 = ((f32[64,2,512]{2,1,0:T(2,128)}), f32[64,2,512]{2,1,0:T(2,128)S(1)}, u32[]{:S(2)}, u32[]{:S(2)}) async-start(f32[64,2,512]{2,1,0:T(2,128)} %broadcast_select_fusion), calls=%async_computation.1 | async-start | bytes 524288 | tf_op jit(solution)/shard_map/all_to_all | solution.py:157
  (11 other events, 23.8 us)
where the time goes:
time: 217 us; the launch traced here: 216 us
  local copies, waits for them, and re-layouts  69.3 us (32%)
  other arithmetic  59.1 us (27%)
  blocking collectives  47.6 us (22%)
  waiting for transfers between devices  22.4 us (10%)
  starting transfers between devices  15.8 us (7%)
    pmax x5, blocking collectives, over_axes(): x = lax.pmax(x, axis)  47.6 us
    sub x3, other arithmetic, face_flux(): return average - 0.5 * signal_speed[None] * (right_state - left_state)  21.4 us
    another operation x4, local copies, waits for them, and re-layouts, physical_flux(): return jnp.stack(pieces, axis=0)  14 us
    all_to_all x1, waiting for transfers between devices, body(): lax.all_to_all(by_column, SLAB, split_axis=1, concat_axis=2, tiled=True)  12.2 us
    slice x4, local copies, waits for them, and re-layouts, body(): first_flux = face_flux(inner_rows[:, :-1], inner_rows[:, 1:], 0)  11.6 us
    all_to_all x1, waiting for transfers between devices, body(): lax.all_to_all(outgoing, SLAB, split_axis=0, concat_axis=0, tiled=True)  10.2 us
    unnamed x17, other arithmetic  8.3 us
    unnamed x59, local copies, waits for them, and re-layouts  8.13 us
  transfers between devices with their start and end apart: 6, of which 2 were waited for; matrix products, arithmetic and copies ran while one was open for 24% of the time, Pallas kernels for 0%

commit v1 on v0

v1 whole, which is shorter than its diff:
```python
import functools
import math

import jax
import jax.numpy as jnp
from jax import lax
from jax.experimental import pallas as pl
from jax.experimental.pallas import tpu as pltpu
from jax.sharding import PartitionSpec as P

MESH = pl.DeviceIdType.MESH
GAMMA = 5.0 / 3.0
COURANT = 0.15
TURBULENT = 0.25
NORMALISE = 0.5641895835477563
NSLAB = 64
NSECT = 4
NXL = 8
CY = 32
NZ = 128
MOST = 4
NX = 512
LOG2E = math.log2(math.e)
F32 = jnp.float32


def state(prim):
    r, v0, v1, v2, p = prim
    m0, m1, m2 = r * v0, r * v1, r * v2
    energy = 1.5 * p + 0.5 * (m0 * v0 + m1 * v1 + m2 * v2)
    return (r, m0, m1, m2, energy)


def sound(prim):
    return jnp.sqrt(GAMMA * (prim[4] / prim[0]))


def side(prim, w, c, d):
    moving, p = prim[1 + d], prim[4]
    flux = [w[1 + d], w[1] * moving, w[2] * moving, w[3] * moving, (w[4] + p) * moving]
    flux[1 + d] = flux[1 + d] + p
    return w, flux, jnp.abs(moving) + c


def face(left, right):
    (wl, fl, al), (wr, fr, ar) = left, right
    a = jnp.maximum(al, ar)
    return [(fl[k] + fr[k]) - a * (wr[k] - wl[k]) for k in range(5)]


def cell(prim, d):
    return side(prim, state(prim), sound(prim), d)


def iota(shape, dim):
    return lax.broadcasted_iota(jnp.int32, shape, dim)


def comm_kernel(den, vel, pre, own, w_out, d_out, r_out, U, hs, hr, ms, mr, cs, xs, oh, ps, in_sem, hs_sem, hr_sem, xs_sem, xr_sem,
                loc_sem, as_sem, ar_sem):
    me = lax.axis_index("slab")
    sect = lax.axis_index("sect")

    inner = (pl.ds(1, NXL), pl.ds(8, CY))
    copies = [
        pltpu.make_async_copy(den, U.at[(0,) + inner], in_sem.at[0]),
        pltpu.make_async_copy(vel, U.at[(pl.ds(1, 3),) + inner], in_sem.at[1]),
        pltpu.make_async_copy(pre, U.at[(4,) + inner], in_sem.at[2]),
    ]
    for c in copies:
        c.start()

    barrier = pltpu.get_barrier_semaphore()

    def greet(i, carry):
        pl.semaphore_signal(barrier, inc=1, device_id={"slab": lax.rem(me + i, NSLAB)}, device_id_type=MESH)
        return carry

    lax.fori_loop(1, NSLAB, greet, 0)
    for i in range(1, NSECT):
        pl.semaphore_signal(barrier, inc=1, device_id={"sect": lax.rem(sect + i, NSECT)}, device_id_type=MESH)

    row = jnp.concatenate([own[k].astype(F32) for k in range(4)], axis=1)
    across = jnp.broadcast_to(row, (128, 128))
    down = jnp.transpose(across)
    lane, sub = iota((128, 128), 1), iota((128, 128), 0)
    count = lambda i: lax.rem(i, 32) * 4 + i // 32
    earlier = jnp.where((across == down) & (count(sub) < count(lane)), 1.0, 0.0)
    rank = jnp.sum(earlier, axis=0, keepdims=True)
    target = row * MOST + rank
    slots = iota((NSLAB * MOST, 128), 0).astype(F32)
    oh[...] = jnp.where(slots == target, 1.0, 0.0).astype(jnp.bfloat16)

    for c in copies:
        c.wait()

    def local_max(x, best):
        for yb in range(4):
            prim = [U[f, x + 1, 8 + 8 * yb:16 + 8 * yb, :] for f in range(5)]
            top = jnp.maximum(jnp.maximum(jnp.abs(prim[1]), jnp.abs(prim[2])), jnp.abs(prim[3])) + sound(prim)
            best = jnp.maximum(best, top)
        return best

    best = lax.fori_loop(0, NXL, local_max, jnp.zeros((8, 128), F32))
    best = jnp.broadcast_to(jnp.max(best, keepdims=True), (8, 128))
    ms[...] = best
    for f in range(5):
        hs[0, f] = U[f, 1:9, 39, :]
        hs[1, f] = U[f, 1:9, 8, :]
    hs[0, 5] = best
    hs[1, 5] = best

    pl.semaphore_wait(barrier, NSLAB - 1 + NSECT - 1)

    def remote(src, dst, ssem, rsem, where):
        return pltpu.make_async_remote_copy(src_ref=src, dst_ref=dst, send_sem=ssem, recv_sem=rsem, device_id=where,
                                            device_id_type=MESH)

    near = [
        remote(hs.at[0], hr.at[0], hs_sem.at[0], hr_sem.at[0], {"sect": lax.rem(sect + 1, NSECT)}),
        remote(hs.at[1], hr.at[1], hs_sem.at[1], hr_sem.at[1], {"sect": lax.rem(sect + NSECT - 1, NSECT)}),
        remote(ms, mr, hs_sem.at[2], hr_sem.at[2], {"sect": lax.rem(sect + 2, NSECT)}),
    ]
    ends = [
        remote(U.at[:, 8, pl.ds(8, CY)], U.at[:, 0, pl.ds(8, CY)], xs_sem.at[0], xr_sem.at[0], {"slab": lax.rem(me + 1, NSLAB)}),
        remote(U.at[:, 1, pl.ds(8, CY)], U.at[:, 9, pl.ds(8, CY)], xs_sem.at[1], xr_sem.at[1],
               {"slab": lax.rem(me + NSLAB - 1, NSLAB)}),
    ]
    for c in near:
        c.start()
    for c in ends:
        c.start()

    wide = iota((CY, 128), 1)
    wide32 = lax.rem(wide, 32)
    for f in range(5):
        packed = jnp.ones((CY, 128), F32)
        for x in range(NXL):
            tile = U[f, x + 1, 8:40, :]
            for step in (-1, 0, 1):
                n = x + 8 * (step + 1)
                shift = (n - step) % 128
                packed = jnp.where(wide32 == n, pltpu.roll(tile, shift, 1) if shift else tile, packed)
        cs[f, 8:40, :] = packed

    for c in near:
        c.wait_recv()
    best = jnp.maximum(jnp.maximum(best, hr[0, 5]), jnp.maximum(hr[1, 5], mr[...]))
    l8, s8 = iota((8, 128), 1), iota((8, 128), 0)
    pick = lax.rem(l8, 32) == s8 + 8
    for f in range(5):
        for way, to in ((0, 7), (1, 40)):
            turned = pltpu.roll(hr[way, f], 8, 1, stride=1, stride_axis=0)
            cs[f, to:to + 1, :] = jnp.sum(jnp.where(pick, turned, 0.0), axis=0, keepdims=True)

    l8_32 = lax.rem(l8, 32)
    middle = (l8_32 >= 8) & (l8_32 < 16)
    for yb in range(4):
        here = [cs[f, 8 + 8 * yb:16 + 8 * yb, :] for f in range(5)]
        above = [cs[f, 9 + 8 * yb:17 + 8 * yb, :] for f in range(5)]
        below = [cs[f, 7 + 8 * yb:15 + 8 * yb, :] for f in range(5)]
        w, c = state(here), sound(here)
        nextz = [pltpu.roll(a, 120, 1) for a in here]
        fz = face(side(here, w, c, 2), cell(nextz, 2))
        mid = side(here, w, c, 1)
        fu, fd = face(mid, cell(above, 1)), face(cell(below, 1), mid)
        moved = [(fu[k] - fd[k]) + (fz[k] - pltpu.roll(fz[k], 8, 1)) for k in range(5)]
        items = [jnp.where(middle, a, 0.0) for a in list(here) + moved]
        groups = []
        for g in range(3):
            total = None
            for j, item in enumerate(items[4 * g:4 * g + 4]):
                shift = (8 * j - 8) % 128
                part = pltpu.roll(item, shift, 1) if shift else item
                total = part if total is None else total + part
            groups.append(total)
        for k in range(4):
            block = jnp.zeros((8, 128), F32)
            for g in range(3):
                shift = (32 * g - 32 * k) % 128
                part = pltpu.roll(groups[g], shift, 1) if shift else groups[g]
                block = jnp.where(l8 // 32 == g, part, block)
            xs[32 * k + 8 * yb:32 * k + 8 * yb + 8, :] = block

    lines = xs[...]
    hi = lines.astype(jnp.bfloat16)
    rest = lines - hi.astype(F32)
    mid = rest.astype(jnp.bfloat16)
    lo = (rest - mid.astype(F32)).astype(jnp.bfloat16)
    chosen = oh[...]
    dot = functools.partial(jnp.dot, preferred_element_type=F32)
    sent = dot(chosen, hi) + (dot(chosen, mid) + dot(chosen, lo))
    sent = jnp.where(iota((NSLAB * MOST, 128), 1) >= 80, jnp.broadcast_to(best[0:1, :], (NSLAB * MOST, 128)), sent)
    ps[...] = sent.reshape(NSLAB, MOST, 128)

    def deliver(i, carry):
        q = lax.rem(me + i, NSLAB)
        remote(ps.at[q], r_out.at[me], as_sem, ar_sem, {"slab": q}).start()
        return carry

    lax.fori_loop(1, NSLAB, deliver, 0)
    mine = pltpu.make_async_copy(ps.at[me], r_out.at[me], loc_sem)
    mine.start()

    for f in range(5):
        U[f, 1:9, 7, :] = hr[0, f]
        U[f, 1:9, 40, :] = hr[1, f]
    for c in ends:
        c.wait_recv()

    def dense(x, carry):
        for yb in range(4):
            lo, hi = 8 + 8 * yb, 16 + 8 * yb
            here = [U[f, x + 1, lo:hi, :] for f in range(5)]
            w, c = state(here), sound(here)
            fz = face(side(here, w, c, 2), cell([pltpu.roll(a, 127, 1) for a in here], 2))
            moved = [fz[k] - pltpu.roll(fz[k], 1, 1) for k in range(5)]
            for d, pair in ((1, ((1, 1), (1, -1))), (0, ((2, 0), (0, 0)))):
                (xu, yu), (xd, yd) = pair
                mid = side(here, w, c, d)
                fu = face(mid, cell([U[f, x + xu, lo + yu:hi + yu, :] for f in range(5)], d))
                fd = face(cell([U[f, x + xd, lo + yd:hi + yd, :] for f in range(5)], d), mid)
                moved = [moved[k] + (fu[k] - fd[k]) for k in range(5)]
            for k in range(5):
                w_out[k, x, lo - 8:hi - 8, :] = w[k]
                d_out[k, x, lo - 8:hi - 8, :] = moved[k]
        return carry

    lax.fori_loop(0, NXL, dense, 0)

    mine.wait()
    for c in near + ends:
        c.wait_send()
    most = pl.ds(0, NSLAB - 1)
    pltpu.make_async_copy(ps.at[most], ps.at[most], as_sem).wait()
    pltpu.make_async_copy(r_out.at[most], r_out.at[most], ar_sem).wait()


def final_kernel(w_ref, d_ref, r_ref, own, new_hbm, od, nb, table, sem):
    me = lax.axis_index("slab").astype(F32)
    arrived = r_ref[...]
    fastest = jnp.max(jnp.max(arrived, axis=0), axis=0, keepdims=True)[:, 96:97]
    half_dt = (0.5 * COURANT) / fastest
    hdt = jnp.broadcast_to(half_dt, (8, 128))

    def advance(x, carry):
        for k in range(5):
            for yb in range(4):
                at = (k, x, slice(8 * yb, 8 * yb + 8))
                nb[at] = w_ref[at] - hdt * d_ref[at]
        return carry

    lax.fori_loop(0, NXL, advance, 0)
    out = pltpu.make_async_copy(nb, new_hbm, sem)
    out.start()

    l8, s8 = iota((8, 128), 1), iota((8, 128), 0)
    for u in range(64):
        o = l8 - s8 + 8 * u
        o = jnp.where(o >= NX // 2, o - NX, o)
        table[u] = o.astype(F32)

    turned = jnp.transpose(arrived.reshape(NSLAB * MOST, 128))
    fields = [turned[8 * f:8 * f + 8, :] for f in range(10)]
    here, moved = fields[:5], fields[5:]
    s2 = iota((8, NSLAB * MOST), 0)

    def after(a):
        a = pltpu.roll(a, 7, 0)
        return jnp.where(s2 < 7, a, pltpu.roll(a, NSLAB * MOST - 4, 1))

    def before(a):
        a = pltpu.roll(a, 1, 0)
        return jnp.where(s2 > 0, a, pltpu.roll(a, 4, 1))

    w = state(here)
    fx = face(side(here, w, sound(here), 0), cell([after(a) for a in here], 0))
    hdt2 = jnp.broadcast_to(half_dt, (8, NSLAB * MOST))
    new = [w[k] - hdt2 * (moved[k] + (fx[k] - before(fx[k]))) for k in range(5)]
    r = new[0]
    v = [new[1 + k] / r for k in range(3)]
    p = (GAMMA - 1.0) * (new[4] - 0.5 * (new[1] * v[0] + new[2] * v[1] + new[3] * v[2]))
    broad = TURBULENT + p / r
    inverse = math.sqrt(LOG2E) / (8.0 * jnp.sqrt(broad))
    moved_by = (64.0 * v[0]) * inverse
    level = jnp.log2((NORMALISE / 8.0) * (r * r)) - 1.2 * jnp.log2(broad)

    def some(pb, carry):
        inv, mov, lev, sums = carry
        sums = list(sums)
        for pp in range(8):
            tiles = [table[lax.rem(16 * it + 128 - 8 * pb - pp, 64)] for it in range(4)]
            for t in range(4):
                n = 4 * pp + t
                i_b = jnp.broadcast_to(inv[:, n:n + 1], (8, 128))
                m_b = jnp.broadcast_to(mov[:, n:n + 1], (8, 128))
                l_b = jnp.broadcast_to(lev[:, n:n + 1], (8, 128))
                for it in range(4):
                    z = tiles[it] * i_b - m_b
                    sums[4 * t + it] = sums[4 * t + it] + jnp.exp2(l_b - z * z)
        turn = lambda a: pltpu.roll(a, NSLAB * MOST - 32, 1)
        return turn(inv), turn(mov), turn(lev), tuple(sums)

    zero = jnp.zeros((8, 128), F32)
    sums = lax.fori_loop(0, 8, some, (inverse, moved_by, level, (zero,) * 16))[3]
    row = jnp.concatenate([own[k].astype(F32) for k in range(4)], axis=1)
    held = jnp.sum(jnp.where(row == me, 1.0, 0.0), axis=1, keepdims=True)
    for t in range(4):
        line = jnp.concatenate([jnp.sum(sums[4 * t + it], axis=0, keepdims=True) for it in range(4)], axis=1)
        od[0, 0, t:t + 1, :] = jnp.where(held > t, line, 0.0)
    out.wait()


def body(density, velocity, pressure, owners):
    own = jnp.transpose(owners, (1, 2, 0))
    vmem = pl.BlockSpec(memory_space=pltpu.VMEM)
    anyspace = pl.BlockSpec(memory_space=pl.ANY)
    dense = jax.ShapeDtypeStruct((5, NXL, CY, NZ), F32)
    arrived = jax.ShapeDtypeStruct((NSLAB, MOST, 128), F32)
    dma = pltpu.SemaphoreType.DMA
    w, d, r = pl.pallas_call(
        comm_kernel,
        out_shape=(dense, dense, arrived),
        in_specs=[anyspace, anyspace, anyspace, vmem],
        out_specs=(vmem, vmem, vmem),
        scratch_shapes=[
            pltpu.VMEM((5, NXL + 2, CY + 16, NZ), F32),
            pltpu.VMEM((2, 6, 8, 128), F32),
            pltpu.VMEM((2, 6, 8, 128), F32),
            pltpu.VMEM((8, 128), F32),
            pltpu.VMEM((8, 128), F32),
            pltpu.VMEM((5, CY + 16, 128), F32),
            pltpu.VMEM((128, 128), F32),
            pltpu.VMEM((NSLAB * MOST, 128), jnp.bfloat16),
            pltpu.VMEM((NSLAB, MOST, 128), F32),
            dma((3,)), dma((3,)), dma((3,)), dma((2,)), dma((2,)), dma, dma, dma,
        ],
        compiler_params=pltpu.CompilerParams(collective_id=0, has_side_effects=True, vmem_limit_bytes=24 << 20),
        name="exchange",
    )(density, velocity, pressure, own)
    return tuple(pl.pallas_call(
        final_kernel,
        out_shape=(dense, jax.ShapeDtypeStruct((1, 1, MOST, NX), F32)),
        in_specs=[vmem] * 4,
        out_specs=(anyspace, vmem),
        scratch_shapes=[pltpu.VMEM((5, NXL, CY, NZ), F32), pltpu.VMEM((64, 8, 128), F32), dma],
        compiler_params=pltpu.CompilerParams(vmem_limit_bytes=24 << 20),
        name="finish",
    )(w, d, r, own))


def solution(mesh):
    placed = (P("slab", "sect", None), P(None, "slab", "sect", None), P("slab", "sect", None), P("sect", None, None))
    return jax.shard_map(body, mesh=mesh, in_specs=placed, out_specs=(P(None, "slab", "sect", None), P("sect", "slab", None, None)),
                         check_vma=False)
```

time: 217 us -> 29.7 us (0.14)
  the two profiles are of different devices: /device:TPU:32 before, /device:TPU:1 now
where the time goes in v1:
time: 29.7 us; the launch traced here: 29.5 us
  Pallas kernels  25.4 us (86%)
  local copies, waits for them, and re-layouts  3.48 us (12%)
  between operations  0.65 us (2%)
    pallas_call x1, Pallas kernels, body(): pl.pallas_call(comm_kernel, out_shape=(dense, dense, arrived), in_specs=[...  22.3 us
    unnamed x8, local copies, waits for them, and re-layouts  3.48 us
    pallas_call x1, Pallas kernels, body(): pl.pallas_call(final_kernel, out_shape=(dense, jax.ShapeDtypeStruct((1, 1...  3.06 us

profile of v1, /device:TPU:1, one launch (start us, length us, event | category | flops | bytes accessed | tf_op | source)
XLA Modules:
  0.0 29.5 jit_solution(7825481910782761812)
XLA Ops:
  0.6 0.0 copy-start
  0.6 1.0 %copy-done = f32[3,8,32,128]{3,2,1,0:T(8,128)S(1)} copy-done((f32[3,8,32,128]{3,2,1,0:T(8,128)S(1)}, f32[3,8,32,128]{3,2,1,0:T(8,128)}, u32[]{:S(2)}) %copy-start) | copy-done | bytes 393240
  1.6 0.0 copy-start.1
  1.6 0.9 %copy-done.1 = f32[8,32,128]{2,1,0:T(8,128)S(1)} copy-done((f32[8,32,128]{2,1,0:T(8,128)S(1)}, f32[8,32,128]{2,1,0:T(8,128)}, u32[]{:S(2)}) %copy-start.1) | copy-done | bytes 131096
  2.5 0.0 copy-start.2
  2.5 0.9 %copy-done.2 = f32[8,32,128]{2,1,0:T(8,128)S(1)} copy-done((f32[8,32,128]{2,1,0:T(8,128)S(1)}, f32[8,32,128]{2,1,0:T(8,128)}, u32[]{:S(2)}) %copy-start.2) | copy-done | bytes 131096
  3.4 0.0 copy-start.3
  3.4 0.7 %copy-done.3 = s32[32,4,1]{0,2,1:T(1,128)S(1)} copy-done((s32[32,4,1]{0,2,1:T(1,128)S(1)}, s32[32,4,1]{0,2,1:T(1,128)}, u32[]{:S(2)}) %copy-start.3) | copy-done | bytes 536
  4.1 22.3 %exchange.1 = (f32[5,8,32,128]{3,2,1,0:T(8,128)S(1)}, f32[5,8,32,128]{3,2,1,0:T(8,128)S(1)}, f32[64,4,128]{2,1,0:T(4,128)S(1)}) custom-call(f32[8,32,128]{2,1,0:T(8,128)S(1)} %copy-done.1, f32[3,8,32,128]{3,2,1,0:T(8,128)S(1)} %copy-done, f32[8,32,128]{2,1,0:T(8,128)S(1)} %copy-done.2, s32[4,1,32]{2,1,0:T(1,128)S(1)} %bitcast.1), custom_call_target="tpu_custom_call" | custom-call | tf_op jit(solution)/shard_map/exchange/pallas_call | solution.py:321
  26.5 3.1 %finish.1 = (f32[5,8,32,128]{3,2,1,0:T(8,128)}, f32[1,1,4,512]{3,2,1,0:T(4,128)}) custom-call(f32[5,8,32,128]{3,2,1,0:T(8,128)S(1)} %get-tuple-element.5.w_ref, f32[5,8,32,128]{3,2,1,0:T(8,128)S(1)} %get-tuple-element.6.d_ref, f32[64,4,128]{2,1,0:T(4,128)S(1)} %get-tuple-element.7.r_ref, s32[4,1,32]{2,1,0:T(1,128)S(1)} %bitcast.2), custom_call_target="tpu_custom_call" | custom-call | tf_op jit(solution)/shard_map/finish/pallas_call | solution.py:341
Async XLA Ops:
  0.6 1.0 %copy-start = (f32[3,8,32,128]{3,2,1,0:T(8,128)S(1)}, f32[3,8,32,128]{3,2,1,0:T(8,128)}, u32[]{:S(2)}) copy-start(f32[3,8,32,128]{3,2,1,0:T(8,128)} %vel.1) | copy-start | bytes 1179652
  1.6 0.9 %copy-start.1 = (f32[8,32,128]{2,1,0:T(8,128)S(1)}, f32[8,32,128]{2,1,0:T(8,128)}, u32[]{:S(2)}) copy-start(f32[8,32,128]{2,1,0:T(8,128)} %den.1) | copy-start | bytes 393220
  2.5 0.9 %copy-start.2 = (f32[8,32,128]{2,1,0:T(8,128)S(1)}, f32[8,32,128]{2,1,0:T(8,128)}, u32[]{:S(2)}) copy-start(f32[8,32,128]{2,1,0:T(8,128)} %pre.1) | copy-start | bytes 393220
  3.4 0.7 %copy-start.3 = (s32[32,4,1]{0,2,1:T(1,128)S(1)}, s32[32,4,1]{0,2,1:T(1,128)}, u32[]{:S(2)}) copy-start(s32[32,4,1]{0,2,1:T(1,128)} %param.7) | copy-start | bytes 1540

commit v2 on v1

--- a/solution.py
+++ b/solution.py
@@ -20,8 +20,9 @@
 NZ = 128
 MOST = 4
 NX = 512
+F32 = jnp.float32
 LOG2E = math.log2(math.e)
-F32 = jnp.float32
+RINGS = ((1, 2), (1, 1), (1, 3), (0, 2), (1, 0), (0, 1), (0, 3))
 
 
 def state(prim):
@@ -56,11 +57,14 @@
     return lax.broadcasted_iota(jnp.int32, shape, dim)
 
 
-def comm_kernel(den, vel, pre, own, w_out, d_out, r_out, U, hs, hr, ms, mr, cs, xs, oh, ps, in_sem, hs_sem, hr_sem, xs_sem, xr_sem,
-                loc_sem, as_sem, ar_sem):
+def comm_kernel(den, vel, pre, own_hbm, w_out, d_out, r_out, table, U, hs, hr, cm, cr, ms, mr, cs, xs, oh, ps, own, in_sem, hs_sem,
+                hr_sem, xs_sem, xr_sem, loc_sem, as_sem, ar_sem, back, go):
     me = lax.axis_index("slab")
     sect = lax.axis_index("sect")
-
+    far, row_y, row_z = me // 32, lax.rem(me // 8, 4), lax.rem(me, 8)
+    low, high = row_z < 4, row_z >= 4
+
+    owned = pltpu.make_async_copy(own_hbm, own, in_sem.at[3])
     inner = (pl.ds(1, NXL), pl.ds(8, CY))
     copies = [
         pltpu.make_async_copy(den, U.at[(0,) + inner], in_sem.at[0]),
@@ -69,17 +73,36 @@
     ]
     for c in copies:
         c.start()
+    owned.start()
+
+    def slab_of(step_x, step_y, z):
+        return lax.rem(far + step_x, 2) * 32 + lax.rem(row_y + step_y, 4) * 8 + z
 
     barrier = pltpu.get_barrier_semaphore()
-
-    def greet(i, carry):
-        pl.semaphore_signal(barrier, inc=1, device_id={"slab": lax.rem(me + i, NSLAB)}, device_id_type=MESH)
-        return carry
-
-    lax.fori_loop(1, NSLAB, greet, 0)
     for i in range(1, NSECT):
         pl.semaphore_signal(barrier, inc=1, device_id={"sect": lax.rem(sect + i, NSECT)}, device_id_type=MESH)
 
+    def tell(sem, q):
+        pl.semaphore_signal(sem, inc=1, device_id={"slab": q}, device_id_type=MESH)
+
+    @pl.when(low)
+    def _():
+        for i in range(1, 4):
+            tell(barrier, slab_of(0, 0, lax.rem(row_z + i, 4)))
+        for i in range(4):
+            tell(barrier, slab_of(0, 0, 4 + i))
+        for a, b in RINGS:
+            for z in range(8):
+                tell(barrier, slab_of(a, b, z))
+
+    @pl.when(high)
+    def _():
+        pl.semaphore_wait(barrier, 35)
+        for a, b in ((0, 0),) + RINGS:
+            for z in range(4):
+                tell(back, slab_of(a, b, z))
+
+    owned.wait()
     row = jnp.concatenate([own[k].astype(F32) for k in range(4)], axis=1)
     across = jnp.broadcast_to(row, (128, 128))
     down = jnp.transpose(across)
@@ -94,6 +117,15 @@
     for c in copies:
         c.wait()
 
+    l8, s8 = iota((8, 128), 1), iota((8, 128), 0)
+    pick = lax.rem(l8, 32) == s8 + 8
+    for f in range(5):
+        for way, y in ((0, 39), (1, 8)):
+            edge = U[f, 1:9, y, :]
+            hs[way, f] = edge
+            turned = pltpu.roll(edge, 8, 1, stride=1, stride_axis=0)
+            cm[way, f:f + 1, :] = jnp.sum(jnp.where(pick, turned, 0.0), axis=0, keepdims=True)
+
     def local_max(x, best):
         for yb in range(4):
             prim = [U[f, x + 1, 8 + 8 * yb:16 + 8 * yb, :] for f in range(5)]
@@ -104,32 +136,42 @@
     best = lax.fori_loop(0, NXL, local_max, jnp.zeros((8, 128), F32))
     best = jnp.broadcast_to(jnp.max(best, keepdims=True), (8, 128))
     ms[...] = best
-    for f in range(5):
-        hs[0, f] = U[f, 1:9, 39, :]
-        hs[1, f] = U[f, 1:9, 8, :]
-    hs[0, 5] = best
-    hs[1, 5] = best
-
-    pl.semaphore_wait(barrier, NSLAB - 1 + NSECT - 1)
+    for way in range(2):
+        cm[way, 5:8, :] = best[5:8, :]
+
+    @pl.when(low)
+    def _():
+        pl.semaphore_wait(barrier, 34)
 
     def remote(src, dst, ssem, rsem, where):
         return pltpu.make_async_remote_copy(src_ref=src, dst_ref=dst, send_sem=ssem, recv_sem=rsem, device_id=where,
                                             device_id_type=MESH)
 
+    above_me, below_me = {"sect": lax.rem(sect + 1, NSECT)}, {"sect": lax.rem(sect + NSECT - 1, NSECT)}
     near = [
-        remote(hs.at[0], hr.at[0], hs_sem.at[0], hr_sem.at[0], {"sect": lax.rem(sect + 1, NSECT)}),
-        remote(hs.at[1], hr.at[1], hs_sem.at[1], hr_sem.at[1], {"sect": lax.rem(sect + NSECT - 1, NSECT)}),
+        remote(cm.at[0], cr.at[0], hs_sem.at[0], hr_sem.at[0], above_me),
+        remote(cm.at[1], cr.at[1], hs_sem.at[1], hr_sem.at[1], below_me),
         remote(ms, mr, hs_sem.at[2], hr_sem.at[2], {"sect": lax.rem(sect + 2, NSECT)}),
     ]
+    sides = [
+        remote(hs.at[0], hr.at[0], hs_sem.at[3], hr_sem.at[3], above_me),
+        remote(hs.at[1], hr.at[1], hs_sem.at[4], hr_sem.at[4], below_me),
+    ]
+    after, before = lax.rem(me + 1, NSLAB), lax.rem(me + NSLAB - 1, NSLAB)
     ends = [
-        remote(U.at[:, 8, pl.ds(8, CY)], U.at[:, 0, pl.ds(8, CY)], xs_sem.at[0], xr_sem.at[0], {"slab": lax.rem(me + 1, NSLAB)}),
-        remote(U.at[:, 1, pl.ds(8, CY)], U.at[:, 9, pl.ds(8, CY)], xs_sem.at[1], xr_sem.at[1],
-               {"slab": lax.rem(me + NSLAB - 1, NSLAB)}),
+        remote(U.at[:, 8, pl.ds(8, CY)], U.at[:, 0, pl.ds(8, CY)], xs_sem.at[0], xr_sem.at[0], {"slab": after}),
+        remote(U.at[:, 1, pl.ds(8, CY)], U.at[:, 9, pl.ds(8, CY)], xs_sem.at[1], xr_sem.at[1], {"slab": before}),
     ]
-    for c in near:
+    for c in near + sides:
         c.start()
-    for c in ends:
-        c.start()
+
+    @pl.when((row_z < 3) | (row_z == 7))
+    def _():
+        ends[0].start()
+
+    @pl.when((row_z > 0) & (row_z < 5))
+    def _():
+        ends[1].start()
 
     wide = iota((CY, 128), 1)
     wide32 = lax.rem(wide, 32)
@@ -145,13 +187,10 @@
 
     for c in near:
         c.wait_recv()
-    best = jnp.maximum(jnp.maximum(best, hr[0, 5]), jnp.maximum(hr[1, 5], mr[...]))
-    l8, s8 = iota((8, 128), 1), iota((8, 128), 0)
-    pick = lax.rem(l8, 32) == s8 + 8
+    best = jnp.maximum(jnp.maximum(best[5:6, :], cr[0, 5:6, :]), jnp.maximum(cr[1, 5:6, :], mr[5:6, :]))
     for f in range(5):
-        for way, to in ((0, 7), (1, 40)):
-            turned = pltpu.roll(hr[way, f], 8, 1, stride=1, stride_axis=0)
-            cs[f, to:to + 1, :] = jnp.sum(jnp.where(pick, turned, 0.0), axis=0, keepdims=True)
+        cs[f, 7:8, :] = cr[0, f:f + 1, :]
+        cs[f, 40:41, :] = cr[1, f:f + 1, :]
 
     l8_32 = lax.rem(l8, 32)
     middle = (l8_32 >= 8) & (l8_32 < 16)
@@ -190,23 +229,78 @@
     chosen = oh[...]
     dot = functools.partial(jnp.dot, preferred_element_type=F32)
     sent = dot(chosen, hi) + (dot(chosen, mid) + dot(chosen, lo))
-    sent = jnp.where(iota((NSLAB * MOST, 128), 1) >= 80, jnp.broadcast_to(best[0:1, :], (NSLAB * MOST, 128)), sent)
+    sent = jnp.where(iota((NSLAB * MOST, 128), 1) >= 80, jnp.broadcast_to(best, (NSLAB * MOST, 128)), sent)
     ps[...] = sent.reshape(NSLAB, MOST, 128)
 
-    def deliver(i, carry):
-        q = lax.rem(me + i, NSLAB)
+    def deliver(q):
         remote(ps.at[q], r_out.at[me], as_sem, ar_sem, {"slab": q}).start()
-        return carry
-
-    lax.fori_loop(1, NSLAB, deliver, 0)
+
+    def deliver_half(base):
+        for a, b in RINGS:
+            for z in range(4):
+                deliver(slab_of(a, b, base + z))
+
+    def deliver_own_ring(base):
+        for i in range(1, 4):
+            deliver(slab_of(0, 0, base + lax.rem(row_z + i, 4)))
+
+    def deliver_other_ring(base):
+        for z in range(4):
+            deliver(slab_of(0, 0, base + z))
+
+    @pl.when(low)
+    def _():
+        deliver_half(0)
+        deliver_own_ring(0)
+
+        pl.semaphore_wait(back, NSLAB // 2)
+
+        @pl.when(row_z == 3)
+        def _():
+            tell(go, slab_of(0, 0, 4))
+            tell(go, slab_of(0, 0, 5))
+            ends[0].start()
+
+        @pl.when(row_z == 0)
+        def _():
+            tell(go, slab_of(0, 0, 6))
+            tell(go, slab_of(0, 0, 7))
+            ends[1].start()
+
+        deliver_half(4)
+        deliver_other_ring(4)
+
+    @pl.when(high)
+    def _():
+        deliver_half(0)
+        deliver_other_ring(0)
+
+        pl.semaphore_wait(go, 1)
+
+        @pl.when(row_z < 7)
+        def _():
+            ends[0].start()
+
+        @pl.when(row_z > 4)
+        def _():
+            ends[1].start()
+
+        deliver_half(4)
+        deliver_own_ring(4)
+
     mine = pltpu.make_async_copy(ps.at[me], r_out.at[me], loc_sem)
     mine.start()
 
+    for u in range(65):
+        o = s8 + (8 * u - 8) - 8 * (l8 // 4)
+        o = jnp.where(o >= NX // 2, o - NX, o)
+        table[8 * u:8 * u + 8, :] = o.astype(F32)
+
+    for c in sides:
+        c.wait_recv()
     for f in range(5):
         U[f, 1:9, 7, :] = hr[0, f]
         U[f, 1:9, 40, :] = hr[1, f]
-    for c in ends:
-        c.wait_recv()
 
     def dense(x, carry):
         for yb in range(4):
@@ -226,18 +320,23 @@
                 d_out[k, x, lo - 8:hi - 8, :] = moved[k]
         return carry
 
-    lax.fori_loop(0, NXL, dense, 0)
+    lax.fori_loop(1, NXL - 1, dense, 0)
+    for c in ends:
+        c.wait_recv()
+    lax.fori_loop(0, 2, lambda i, carry: dense((NXL - 1) * i, carry), 0)
 
     mine.wait()
-    for c in near + ends:
+    for c in near + sides + ends:
         c.wait_send()
     most = pl.ds(0, NSLAB - 1)
     pltpu.make_async_copy(ps.at[most], ps.at[most], as_sem).wait()
     pltpu.make_async_copy(r_out.at[most], r_out.at[most], ar_sem).wait()
 
 
-def final_kernel(w_ref, d_ref, r_ref, own, new_hbm, od, nb, table, sem):
+def final_kernel(w_ref, d_ref, r_ref, table, own_hbm, new_hbm, od, nb, pb, acc, own, sem, own_sem):
     me = lax.axis_index("slab").astype(F32)
+    owned = pltpu.make_async_copy(own_hbm, own, own_sem)
+    owned.start()
     arrived = r_ref[...]
     fastest = jnp.max(jnp.max(arrived, axis=0), axis=0, keepdims=True)[:, 96:97]
     half_dt = (0.5 * COURANT) / fastest
@@ -253,12 +352,6 @@
     lax.fori_loop(0, NXL, advance, 0)
     out = pltpu.make_async_copy(nb, new_hbm, sem)
     out.start()
-
-    l8, s8 = iota((8, 128), 1), iota((8, 128), 0)
-    for u in range(64):
-        o = l8 - s8 + 8 * u
-        o = jnp.where(o >= NX // 2, o - NX, o)
-        table[u] = o.astype(F32)
 
     turned = jnp.transpose(arrived.reshape(NSLAB * MOST, 128))
     fields = [turned[8 * f:8 * f + 8, :] for f in range(10)]
@@ -284,56 +377,67 @@
     inverse = math.sqrt(LOG2E) / (8.0 * jnp.sqrt(broad))
     moved_by = (64.0 * v[0]) * inverse
     level = jnp.log2((NORMALISE / 8.0) * (r * r)) - 1.2 * jnp.log2(broad)
-
-    def some(pb, carry):
-        inv, mov, lev, sums = carry
-        sums = list(sums)
-        for pp in range(8):
-            tiles = [table[lax.rem(16 * it + 128 - 8 * pb - pp, 64)] for it in range(4)]
-            for t in range(4):
-                n = 4 * pp + t
-                i_b = jnp.broadcast_to(inv[:, n:n + 1], (8, 128))
-                m_b = jnp.broadcast_to(mov[:, n:n + 1], (8, 128))
-                l_b = jnp.broadcast_to(lev[:, n:n + 1], (8, 128))
-                for it in range(4):
-                    z = tiles[it] * i_b - m_b
-                    sums[4 * t + it] = sums[4 * t + it] + jnp.exp2(l_b - z * z)
-        turn = lambda a: pltpu.roll(a, NSLAB * MOST - 32, 1)
-        return turn(inv), turn(mov), turn(lev), tuple(sums)
-
-    zero = jnp.zeros((8, 128), F32)
-    sums = lax.fori_loop(0, 8, some, (inverse, moved_by, level, (zero,) * 16))[3]
+    for n, param in enumerate((inverse, moved_by, level)):
+        for h in range(2):
+            for x in range(8):
+                pb[n, 8 * h + x] = jnp.broadcast_to(param[x:x + 1, 128 * h:128 * h + 128], (8, 128))
+
+    def pixels(block, carry):
+        sums = [None] * 4
+        for h in range(2):
+            for x in range(8):
+                inv, mov, lev = (pb[n, 8 * h + x] for n in range(3))
+                for j in range(4):
+                    u = lax.rem(4 * block + (j + 32 * h), 64)
+                    o = table[pl.ds(8 * u + (8 - x), 8), :]
+                    z = o * inv - mov
+                    part = jnp.exp2(lev - z * z)
+                    sums[j] = part if sums[j] is None else sums[j] + part
+        for j in range(4):
+            acc[pl.ds(pl.multiple_of(32 * block + 8 * j, 8), 8), :] = sums[j]
+        return carry
+
+    lax.fori_loop(0, 16, pixels, 0)
+    depth = jnp.transpose(acc[...])
+    both = depth[0:8, :]
+    for n in range(1, 16):
+        both = both + depth[8 * n:8 * n + 8, :]
+    owned.wait()
     row = jnp.concatenate([own[k].astype(F32) for k in range(4)], axis=1)
     held = jnp.sum(jnp.where(row == me, 1.0, 0.0), axis=1, keepdims=True)
-    for t in range(4):
-        line = jnp.concatenate([jnp.sum(sums[4 * t + it], axis=0, keepdims=True) for it in range(4)], axis=1)
-        od[0, 0, t:t + 1, :] = jnp.where(held > t, line, 0.0)
+    valid = iota((4, NX), 0).astype(F32) < held
+    od[0, 0] = jnp.where(valid, both[0:4, :] + both[4:8, :], 0.0)
     out.wait()
 
 
 def body(density, velocity, pressure, owners):
     own = jnp.transpose(owners, (1, 2, 0))
+    density, velocity, pressure, own = (pltpu.with_memory_space_constraint(a, pltpu.HBM) for a in (density, velocity, pressure, own))
     vmem = pl.BlockSpec(memory_space=pltpu.VMEM)
-    anyspace = pl.BlockSpec(memory_space=pl.ANY)
+    hbm = pl.BlockSpec(memory_space=pltpu.HBM)
     dense = jax.ShapeDtypeStruct((5, NXL, CY, NZ), F32)
     arrived = jax.ShapeDtypeStruct((NSLAB, MOST, 128), F32)
-    dma = pltpu.SemaphoreType.DMA
-    w, d, r = pl.pallas_call(
+    offsets = jax.ShapeDtypeStruct((NX + 8, 128), F32)
+    dma, regular = pltpu.SemaphoreType.DMA, pltpu.SemaphoreType.REGULAR
+    w, d, r, table = pl.pallas_call(
         comm_kernel,
-        out_shape=(dense, dense, arrived),
-        in_specs=[anyspace, anyspace, anyspace, vmem],
-        out_specs=(vmem, vmem, vmem),
+        out_shape=(dense, dense, arrived, offsets),
+        in_specs=[hbm, hbm, hbm, hbm],
+        out_specs=(vmem, vmem, vmem, vmem),
         scratch_shapes=[
             pltpu.VMEM((5, NXL + 2, CY + 16, NZ), F32),
-            pltpu.VMEM((2, 6, 8, 128), F32),
-            pltpu.VMEM((2, 6, 8, 128), F32),
+            pltpu.VMEM((2, 5, 8, 128), F32),
+            pltpu.VMEM((2, 5, 8, 128), F32),
+            pltpu.VMEM((2, 8, 128), F32),
+            pltpu.VMEM((2, 8, 128), F32),
             pltpu.VMEM((8, 128), F32),
             pltpu.VMEM((8, 128), F32),
             pltpu.VMEM((5, CY + 16, 128), F32),
             pltpu.VMEM((128, 128), F32),
             pltpu.VMEM((NSLAB * MOST, 128), jnp.bfloat16),
             pltpu.VMEM((NSLAB, MOST, 128), F32),
-            dma((3,)), dma((3,)), dma((3,)), dma((2,)), dma((2,)), dma, dma, dma,
+            pltpu.VMEM((4, 1, CY), jnp.int32),
+            dma((4,)), dma((5,)), dma((5,)), dma((2,)), dma((2,)), dma, dma, dma, regular, regular,
         ],
         compiler_params=pltpu.CompilerParams(collective_id=0, has_side_effects=True, vmem_limit_bytes=24 << 20),
         name="exchange",
@@ -341,12 +445,18 @@
     return tuple(pl.pallas_call(
         final_kernel,
         out_shape=(dense, jax.ShapeDtypeStruct((1, 1, MOST, NX), F32)),
-        in_specs=[vmem] * 4,
-        out_specs=(anyspace, vmem),
-        scratch_shapes=[pltpu.VMEM((5, NXL, CY, NZ), F32), pltpu.VMEM((64, 8, 128), F32), dma],
+        in_specs=[vmem, vmem, vmem, vmem, hbm],
+        out_specs=(hbm, vmem),
+        scratch_shapes=[
+            pltpu.VMEM((5, NXL, CY, NZ), F32),
+            pltpu.VMEM((3, 16, 8, 128), F32),
+            pltpu.VMEM((NX, 128), F32),
+            pltpu.VMEM((4, 1, CY), jnp.int32),
+            dma, dma,
+        ],
         compiler_params=pltpu.CompilerParams(vmem_limit_bytes=24 << 20),
         name="finish",
-    )(w, d, r, own))
+    )(w, d, r, table, own))
 
 
 def solution(mesh):

time: 29.7 us -> 25.1 us (0.85)
  local copies, waits for them, and re-layouts: 3.48 us -> 0 us
  Pallas kernels: 25.4 us -> 24.4 us
    unnamed x8 -> x0, local copies, waits for them, and re-layouts: 3.48 us -> none
    pallas_call x1, Pallas kernels: 22.3 us -> 21.8 us  [body(): pl.pallas_call(comm_kernel, out_shape=(dense, dense, arrived, offsets), i...]
    pallas_call x1, Pallas kernels: 3.06 us -> 2.56 us  [body(): pl.pallas_call(final_kernel, out_shape=(dense, jax.ShapeDtypeStruct((1, 1...]
where the time goes in v2:
time: 25.1 us; the launch traced here: 25 us
  Pallas kernels  24.4 us (97%)
  between operations  0.64 us (3%)
    pallas_call x1, Pallas kernels, body(): pl.pallas_call(comm_kernel, out_shape=(dense, dense, arrived, offsets), i...  21.8 us
    pallas_call x1, Pallas kernels, body(): pl.pallas_call(final_kernel, out_shape=(dense, jax.ShapeDtypeStruct((1, 1...  2.56 us

profile of v2, /device:TPU:1, one launch (start us, length us, event | category | flops | bytes accessed | tf_op | source)
XLA Modules:
  0.0 25.0 jit_solution(6398915516274700605)
XLA Ops:
  0.6 21.8 %exchange.1 = (f32[5,8,32,128]{3,2,1,0:T(8,128)S(1)}, f32[5,8,32,128]{3,2,1,0:T(8,128)S(1)}, f32[64,4,128]{2,1,0:T(4,128)S(1)}, f32[520,128]{1,0:T(8,128)S(1)}) custom-call(f32[8,32,128]{2,1,0:T(8,128)} %den.1, f32[3,8,32,128]{3,2,1,0:T(8,128)} %vel.1, f32[8,32,128]{2,1,0:T(8,128)} %pre.1, s32[4,1,32]{2,1,0:T(1,128)} %bitcast.1), custom_call_target="tpu_custom_call" | custom-call | tf_op jit(solution)/shard_map/exchange/pallas_call | solution.py:422
  22.4 2.6 %finish.1 = (f32[5,8,32,128]{3,2,1,0:T(8,128)}, f32[1,1,4,512]{3,2,1,0:T(4,128)}) custom-call(f32[5,8,32,128]{3,2,1,0:T(8,128)S(1)} %get-tuple-element.6.w_ref, f32[5,8,32,128]{3,2,1,0:T(8,128)S(1)} %get-tuple-element.7.d_ref, f32[64,4,128]{2,1,0:T(4,128)S(1)} %get-tuple-element.8.r_ref, f32[520,128]{1,0:T(8,128)S(1)} %get-tuple-element.9.table, ...), custom_call_target="tpu_custom_call" | custom-call | tf_op jit(solution)/shard_map/finish/pallas_call | solution.py:445

commit v3 on v2

--- a/solution.py
+++ b/solution.py
@@ -58,11 +58,11 @@
 
 
 def comm_kernel(den, vel, pre, own_hbm, w_out, d_out, r_out, table, U, hs, hr, cm, cr, ms, mr, cs, xs, oh, ps, own, in_sem, hs_sem,
-                hr_sem, xs_sem, xr_sem, loc_sem, as_sem, ar_sem, back, go):
+                hr_sem, xs_sem, xr_sem, loc_sem, as_sem, ar_sem, back, last, go):
     me = lax.axis_index("slab")
     sect = lax.axis_index("sect")
     far, row_y, row_z = me // 32, lax.rem(me // 8, 4), lax.rem(me, 8)
-    low, high = row_z < 4, row_z >= 4
+    low, second, third = row_z < 4, (row_z >= 4) & (far == 0), (row_z >= 4) & (far == 1)
 
     owned = pltpu.make_async_copy(own_hbm, own, in_sem.at[3])
     inner = (pl.ds(1, NXL), pl.ds(8, CY))
@@ -85,22 +85,27 @@
     def tell(sem, q):
         pl.semaphore_signal(sem, inc=1, device_id={"slab": q}, device_id_type=MESH)
 
+    def whole_ring(start, z_from):
+        return [start * 32 + lax.rem(row_y + b, 4) * 8 + z for b in (2, 1, 3, 0) for z in range(z_from, z_from + 4)]
+
+    def other_low():
+        return [slab_of(a, b, z) for a, b in RINGS for z in range(4)]
+
+    def other_high():
+        own = [4 + lax.rem(row_z + i, 4) for i in range(1, 4)]
+        return [slab_of(0, b, z) for b in (2, 1, 3) for z in range(4, 8)] + [slab_of(0, 0, z) for z in own]
+
     @pl.when(low)
     def _():
         for i in range(1, 4):
             tell(barrier, slab_of(0, 0, lax.rem(row_z + i, 4)))
-        for i in range(4):
-            tell(barrier, slab_of(0, 0, 4 + i))
-        for a, b in RINGS:
-            for z in range(8):
-                tell(barrier, slab_of(a, b, z))
-
-    @pl.when(high)
-    def _():
-        pl.semaphore_wait(barrier, 35)
-        for a, b in ((0, 0),) + RINGS:
-            for z in range(4):
-                tell(back, slab_of(a, b, z))
+        for q in other_low() + whole_ring(0, 4) + whole_ring(1, 4):
+            tell(barrier, q)
+
+    @pl.when(second)
+    def _():
+        for q in whole_ring(1, 4):
+            tell(barrier, q)
 
     owned.wait()
     row = jnp.concatenate([own[k].astype(F32) for k in range(4)], axis=1)
@@ -139,9 +144,7 @@
     for way in range(2):
         cm[way, 5:8, :] = best[5:8, :]
 
-    @pl.when(low)
-    def _():
-        pl.semaphore_wait(barrier, 34)
+    pl.semaphore_wait(barrier, 34 + (row_z // 4) * (1 + 16 * far))
 
     def remote(src, dst, ssem, rsem, where):
         return pltpu.make_async_remote_copy(src_ref=src, dst_ref=dst, send_sem=ssem, recv_sem=rsem, device_id=where,
@@ -165,11 +168,21 @@
     for c in near + sides:
         c.start()
 
+    @pl.when(second)
+    def _():
+        for q in whole_ring(0, 0) + whole_ring(1, 0):
+            tell(back, q)
+
+    @pl.when(third)
+    def _():
+        for q in whole_ring(0, 0) + whole_ring(1, 0) + whole_ring(0, 4):
+            tell(last, q)
+
     @pl.when((row_z < 3) | (row_z == 7))
     def _():
         ends[0].start()
 
-    @pl.when((row_z > 0) & (row_z < 5))
+    @pl.when((row_z > 0) & (row_z < 4))
     def _():
         ends[1].start()
 
@@ -235,58 +248,74 @@
     def deliver(q):
         remote(ps.at[q], r_out.at[me], as_sem, ar_sem, {"slab": q}).start()
 
-    def deliver_half(base):
-        for a, b in RINGS:
-            for z in range(4):
-                deliver(slab_of(a, b, base + z))
-
-    def deliver_own_ring(base):
-        for i in range(1, 4):
-            deliver(slab_of(0, 0, base + lax.rem(row_z + i, 4)))
-
-    def deliver_other_ring(base):
-        for z in range(4):
-            deliver(slab_of(0, 0, base + z))
-
     @pl.when(low)
     def _():
-        deliver_half(0)
-        deliver_own_ring(0)
-
-        pl.semaphore_wait(back, NSLAB // 2)
-
-        @pl.when(row_z == 3)
+        for q in other_low() + [slab_of(0, 0, lax.rem(row_z + i, 4)) for i in range(1, 4)]:
+            deliver(q)
+        pl.semaphore_wait(back, NSLAB // 4)
+
+        @pl.when((far == 0) & (row_z == 3))
         def _():
             tell(go, slab_of(0, 0, 4))
             tell(go, slab_of(0, 0, 5))
-            ends[0].start()
-
-        @pl.when(row_z == 0)
+
+        @pl.when((far == 0) & (row_z == 0))
         def _():
             tell(go, slab_of(0, 0, 6))
             tell(go, slab_of(0, 0, 7))
+
+        for q in whole_ring(0, 4):
+            deliver(q)
+        pl.semaphore_wait(last, NSLAB // 4)
+
+        @pl.when(row_z == 3)
+        def _():
+            ends[0].start()
+
+        @pl.when(row_z == 0)
+        def _():
             ends[1].start()
 
-        deliver_half(4)
-        deliver_other_ring(4)
-
-    @pl.when(high)
-    def _():
-        deliver_half(0)
-        deliver_other_ring(0)
-
+        for q in whole_ring(1, 4):
+            deliver(q)
+
+    def to_low():
+        for q in [slab_of(a, b, z) for a, b in RINGS + ((0, 0),) for z in range(4)]:
+            deliver(q)
+
+        @pl.when(row_z == 4)
+        def _():
+            ends[1].start()
+
+    def to_own():
+        @pl.when(row_z < 7)
+        def _():
+            ends[0].start()
+
+        @pl.when(row_z > 4)
+        def _():
+            ends[1].start()
+
+        for q in other_high():
+            deliver(q)
+
+    @pl.when(second)
+    def _():
+        to_low()
         pl.semaphore_wait(go, 1)
-
-        @pl.when(row_z < 7)
-        def _():
-            ends[0].start()
-
-        @pl.when(row_z > 4)
-        def _():
-            ends[1].start()
-
-        deliver_half(4)
-        deliver_own_ring(4)
+        to_own()
+        pl.semaphore_wait(last, NSLAB // 4)
+        tell(go, me + 32)
+        for q in whole_ring(1, 4):
+            deliver(q)
+
+    @pl.when(third)
+    def _():
+        to_low()
+        for q in whole_ring(0, 4):
+            deliver(q)
+        pl.semaphore_wait(go, 1)
+        to_own()
 
     mine = pltpu.make_async_copy(ps.at[me], r_out.at[me], loc_sem)
     mine.start()
@@ -342,16 +371,14 @@
     half_dt = (0.5 * COURANT) / fastest
     hdt = jnp.broadcast_to(half_dt, (8, 128))
 
-    def advance(x, carry):
-        for k in range(5):
+    outs = []
+    for k in range(5):
+        for x in range(NXL):
             for yb in range(4):
                 at = (k, x, slice(8 * yb, 8 * yb + 8))
                 nb[at] = w_ref[at] - hdt * d_ref[at]
-        return carry
-
-    lax.fori_loop(0, NXL, advance, 0)
-    out = pltpu.make_async_copy(nb, new_hbm, sem)
-    out.start()
+        outs.append(pltpu.make_async_copy(nb.at[k], new_hbm.at[k], sem.at[k]))
+        outs[-1].start()
 
     turned = jnp.transpose(arrived.reshape(NSLAB * MOST, 128))
     fields = [turned[8 * f:8 * f + 8, :] for f in range(10)]
@@ -383,21 +410,22 @@
                 pb[n, 8 * h + x] = jnp.broadcast_to(param[x:x + 1, 128 * h:128 * h + 128], (8, 128))
 
     def pixels(block, carry):
-        sums = [None] * 4
+        first = pl.multiple_of(64 * block, 64)
+        starts = (first, pl.multiple_of(lax.rem(first + NX // 2, NX), 64))
+        sums = [None] * 8
         for h in range(2):
             for x in range(8):
                 inv, mov, lev = (pb[n, 8 * h + x] for n in range(3))
-                for j in range(4):
-                    u = lax.rem(4 * block + (j + 32 * h), 64)
-                    o = table[pl.ds(8 * u + (8 - x), 8), :]
+                for j in range(8):
+                    o = table[pl.ds(starts[h] + (8 * j + 8 - x), 8), :]
                     z = o * inv - mov
                     part = jnp.exp2(lev - z * z)
                     sums[j] = part if sums[j] is None else sums[j] + part
-        for j in range(4):
-            acc[pl.ds(pl.multiple_of(32 * block + 8 * j, 8), 8), :] = sums[j]
+        for j in range(8):
+            acc[pl.ds(first + 8 * j, 8), :] = sums[j]
         return carry
 
-    lax.fori_loop(0, 16, pixels, 0)
+    lax.fori_loop(0, 8, pixels, 0)
     depth = jnp.transpose(acc[...])
     both = depth[0:8, :]
     for n in range(1, 16):
@@ -407,7 +435,8 @@
     held = jnp.sum(jnp.where(row == me, 1.0, 0.0), axis=1, keepdims=True)
     valid = iota((4, NX), 0).astype(F32) < held
     od[0, 0] = jnp.where(valid, both[0:4, :] + both[4:8, :], 0.0)
-    out.wait()
+    for out in outs:
+        out.wait()
 
 
 def body(density, velocity, pressure, owners):
@@ -437,7 +466,7 @@
             pltpu.VMEM((NSLAB * MOST, 128), jnp.bfloat16),
             pltpu.VMEM((NSLAB, MOST, 128), F32),
             pltpu.VMEM((4, 1, CY), jnp.int32),
-            dma((4,)), dma((5,)), dma((5,)), dma((2,)), dma((2,)), dma, dma, dma, regular, regular,
+            dma((4,)), dma((5,)), dma((5,)), dma((2,)), dma((2,)), dma, dma, dma, regular, regular, regular,
         ],
         compiler_params=pltpu.CompilerParams(collective_id=0, has_side_effects=True, vmem_limit_bytes=24 << 20),
         name="exchange",
@@ -452,7 +481,7 @@
             pltpu.VMEM((3, 16, 8, 128), F32),
             pltpu.VMEM((NX, 128), F32),
             pltpu.VMEM((4, 1, CY), jnp.int32),
-            dma, dma,
+            dma((5,)), dma,
         ],
         compiler_params=pltpu.CompilerParams(vmem_limit_bytes=24 << 20),
         name="finish",

time: 25.1 us -> 24.2 us (0.964)
  Pallas kernels: 24.4 us -> 23.4 us
    pallas_call x1, Pallas kernels: 21.8 us -> 21.2 us  [body(): pl.pallas_call(comm_kernel, out_shape=(dense, dense, arrived, offsets), i...]
    pallas_call x1, Pallas kernels: 2.56 us -> 2.22 us  [body(): pl.pallas_call(final_kernel, out_shape=(dense, jax.ShapeDtypeStruct((1, 1...]
where the time goes in v3:
time: 24.2 us; the launch traced here: 24.1 us
  Pallas kernels  23.4 us (97%)
  between operations  0.64 us (3%)
    pallas_call x1, Pallas kernels, body(): pl.pallas_call(comm_kernel, out_shape=(dense, dense, arrived, offsets), i...  21.2 us
    pallas_call x1, Pallas kernels, body(): pl.pallas_call(final_kernel, out_shape=(dense, jax.ShapeDtypeStruct((1, 1...  2.22 us

profile of v3, /device:TPU:1, one launch (start us, length us, event | category | flops | bytes accessed | tf_op | source)
XLA Modules:
  0.0 24.1 jit_solution(9380278215052257389)
XLA Ops:
  0.6 21.2 %exchange.1 = (f32[5,8,32,128]{3,2,1,0:T(8,128)S(1)}, f32[5,8,32,128]{3,2,1,0:T(8,128)S(1)}, f32[64,4,128]{2,1,0:T(4,128)S(1)}, f32[520,128]{1,0:T(8,128)S(1)}) custom-call(f32[8,32,128]{2,1,0:T(8,128)} %den.1, f32[3,8,32,128]{3,2,1,0:T(8,128)} %vel.1, f32[8,32,128]{2,1,0:T(8,128)} %pre.1, s32[4,1,32]{2,1,0:T(1,128)} %bitcast.1), custom_call_target="tpu_custom_call" | custom-call | tf_op jit(solution)/shard_map/exchange/pallas_call | solution.py:451
  21.8 2.2 %finish.1 = (f32[5,8,32,128]{3,2,1,0:T(8,128)}, f32[1,1,4,512]{3,2,1,0:T(4,128)}) custom-call(f32[5,8,32,128]{3,2,1,0:T(8,128)S(1)} %get-tuple-element.6.w_ref, f32[5,8,32,128]{3,2,1,0:T(8,128)S(1)} %get-tuple-element.7.d_ref, f32[64,4,128]{2,1,0:T(4,128)S(1)} %get-tuple-element.8.r_ref, f32[520,128]{1,0:T(8,128)S(1)} %get-tuple-element.9.table, ...), custom_call_target="tpu_custom_call" | custom-call | tf_op jit(solution)/shard_map/finish/pallas_call | solution.py:474

commit v4 on v2

v4 whole, which is shorter than its diff:
```python
import functools
import math

import jax
import jax.numpy as jnp
from jax import lax
from jax.experimental import pallas as pl
from jax.experimental.pallas import tpu as pltpu
from jax.sharding import PartitionSpec as P

MESH = pl.DeviceIdType.MESH
GAMMA = 5.0 / 3.0
COURANT = 0.15
TURBULENT = 0.25
NORMALISE = 0.5641895835477563
NSLAB = 64
NSECT = 4
NXL = 8
CY = 32
NZ = 128
MOST = 4
NX = 512
F32 = jnp.float32
LOG2E = math.log2(math.e)
HOPS = lambda a, b, c: 2 * a + min(b, 4 - b) + min(c, 8 - c)
PARTNERS = sorted(((a, b, c) for a in range(2) for b in range(4) for c in range(8) if a + b + c), key=lambda o: -HOPS(*o))
HUB = 53
FROM_HUB = sorted((q for q in range(NSLAB) if q != HUB),
                  key=lambda q: HOPS((q // 32 - 1) % 2, (q // 8 % 4 - 2) % 4, (q % 8 - 5) % 8))


def state(prim):
    r, v0, v1, v2, p = prim
    m0, m1, m2 = r * v0, r * v1, r * v2
    energy = 1.5 * p + 0.5 * (m0 * v0 + m1 * v1 + m2 * v2)
    return (r, m0, m1, m2, energy)


def sound(prim):
    return jnp.sqrt(GAMMA * (prim[4] / prim[0]))


def side(prim, w, c, d):
    moving, p = prim[1 + d], prim[4]
    flux = [w[1 + d], w[1] * moving, w[2] * moving, w[3] * moving, (w[4] + p) * moving]
    flux[1 + d] = flux[1 + d] + p
    return w, flux, jnp.abs(moving) + c


def face(left, right):
    (wl, fl, al), (wr, fr, ar) = left, right
    a = jnp.maximum(al, ar)
    return [(fl[k] + fr[k]) - a * (wr[k] - wl[k]) for k in range(5)]


def cell(prim, d):
    return side(prim, state(prim), sound(prim), d)


def iota(shape, dim):
    return lax.broadcasted_iota(jnp.int32, shape, dim)


def comm_kernel(den, vel, pre, own_hbm, w_out, d_out, r_out, table, U, hs, hr, cm, cr, ms, mr, cs, xs, oh, ohc, base, ps, own, in_sem, hs_sem,
                hr_sem, xs_sem, xr_sem, loc_sem, as_sem, ar_sem, go):
    me = lax.axis_index("slab")
    sect = lax.axis_index("sect")
    far, row_y, row_z = me // 32, lax.rem(me // 8, 4), lax.rem(me, 8)
    owned = pltpu.make_async_copy(own_hbm, own, in_sem.at[6])
    copies = []
    for half in range(2):
        some, to = pl.ds(4 * half, 4), (pl.ds(1 + 4 * half, 4), pl.ds(8, CY))
        copies += [
            pltpu.make_async_copy(den.at[some], U.at[(0,) + to], in_sem.at[3 * half]),
            pltpu.make_async_copy(vel.at[:, some], U.at[(pl.ds(1, 3),) + to], in_sem.at[3 * half + 1]),
            pltpu.make_async_copy(pre.at[some], U.at[(4,) + to], in_sem.at[3 * half + 2]),
        ]
    for c in copies:
        c.start()
    owned.start()

    def slab_of(step_x, step_y, z):
        return lax.rem(far + step_x, 2) * 32 + lax.rem(row_y + step_y, 4) * 8 + z

    barrier = pltpu.get_barrier_semaphore()
    for i in range(1, NSECT):
        pl.semaphore_signal(barrier, inc=1, device_id={"sect": lax.rem(sect + i, NSECT)}, device_id_type=MESH)

    def tell(sem, q):
        pl.semaphore_signal(sem, inc=1, device_id={"slab": q}, device_id_type=MESH)

    after, before = lax.rem(me + 1, NSLAB), lax.rem(me + NSLAB - 1, NSLAB)

    @pl.when(me != HUB)
    def _():
        tell(barrier, HUB)

    @pl.when(after != HUB)
    def _():
        tell(barrier, after)

    @pl.when(before != HUB)
    def _():
        tell(barrier, before)

    @pl.when(me == HUB)
    def _():
        pl.semaphore_wait(barrier, NSLAB - 1 + NSECT - 1)
        for q in FROM_HUB:
            tell(go, q)

    best = jnp.zeros((8, 128), F32)
    for half in range(2):
        for c in copies[3 * half:3 * half + 3]:
            c.wait()
        for x in range(4 * half, 4 * half + 4):
            for yb in range(4):
                prim = [U[f, x + 1, 8 + 8 * yb:16 + 8 * yb, :] for f in range(5)]
                top = jnp.maximum(jnp.maximum(jnp.abs(prim[1]), jnp.abs(prim[2])), jnp.abs(prim[3])) + sound(prim)
                best = jnp.maximum(best, top)
    best = jnp.broadcast_to(jnp.max(best, keepdims=True), (8, 128))
    l8, s8 = iota((8, 128), 1), iota((8, 128), 0)
    pick = lax.rem(l8, 32) == s8 + 8
    for f in range(5):
        for way, y in ((0, 39), (1, 8)):
            edge = U[f, 1:9, y, :]
            hs[way, f] = edge
            turned = pltpu.roll(edge, 8, 1, stride=1, stride_axis=0)
            cm[way, f:f + 1, :] = jnp.sum(jnp.where(pick, turned, 0.0), axis=0, keepdims=True)
    for way in range(2):
        cm[way, 5:8, :] = best[5:8, :]
    ms[...] = best

    @pl.when(me != HUB)
    def _():
        pl.semaphore_wait(barrier, NSECT + 1)

    def remote(src, dst, ssem, rsem, where):
        return pltpu.make_async_remote_copy(src_ref=src, dst_ref=dst, send_sem=ssem, recv_sem=rsem, device_id=where,
                                            device_id_type=MESH)

    sects = [{"sect": lax.rem(sect + i, NSECT)} for i in range(NSECT)]
    near = [
        remote(cm.at[0], cr.at[0], hs_sem.at[0], hr_sem.at[0], sects[1]),
        remote(cm.at[1], cr.at[1], hs_sem.at[1], hr_sem.at[1], sects[3]),
        remote(ms, mr, hs_sem.at[2], hr_sem.at[2], sects[2]),
    ]
    sides = [
        remote(hs.at[0], hr.at[0], hs_sem.at[3], hr_sem.at[3], sects[1]),
        remote(hs.at[1], hr.at[1], hs_sem.at[4], hr_sem.at[4], sects[3]),
    ]
    ends = [
        remote(U.at[:, 8, pl.ds(8, CY)], U.at[:, 0, pl.ds(8, CY)], xs_sem.at[0], xr_sem.at[0], {"slab": after}),
        remote(U.at[:, 1, pl.ds(8, CY)], U.at[:, 9, pl.ds(8, CY)], xs_sem.at[1], xr_sem.at[1], {"slab": before}),
    ]
    for c in near + sides + ends:
        c.start()

    owned.wait()
    row = jnp.concatenate([own[k].astype(F32) for k in range(4)], axis=1)
    across = jnp.broadcast_to(row, (128, 128))
    down = jnp.transpose(across)
    lane, sub = iota((128, 128), 1), iota((128, 128), 0)
    count = lambda i: lax.rem(i, 32) * 4 + i // 32
    earlier = jnp.where((across == down) & (count(sub) < count(lane)), 1.0, 0.0)
    rank = jnp.sum(earlier, axis=0, keepdims=True)
    target = row * MOST + rank
    slots = iota((NSLAB * MOST, 128), 0).astype(F32)
    oh[...] = jnp.where(slots == target, 1.0, 0.0).astype(jnp.bfloat16)
    target8, edges = jnp.broadcast_to(target, (8, 128)), jnp.full((8, 128), -1.0, F32)
    for part in range(3):
        for k in range(4):
            for e in range(2):
                to, source = 32 * part + 8 * k + e, 32 * k + 31 * e
                shift = (to - source) % 128
                edges = jnp.where(l8 == to, pltpu.roll(target8, shift, 1) if shift else target8, edges)
    ohc[...] = jnp.where(slots == edges[0:1, :], 1.0, 0.0).astype(jnp.bfloat16)

    wide = iota((CY, 128), 1)
    wide32 = lax.rem(wide, 32)
    for f in range(5):
        packed = jnp.ones((CY, 128), F32)
        for x in range(NXL):
            tile = U[f, x + 1, 8:40, :]
            for step in (-1, 0, 1):
                n = x + 8 * (step + 1)
                shift = (n - step) % 128
                packed = jnp.where(wide32 == n, pltpu.roll(tile, shift, 1) if shift else tile, packed)
        cs[f, 8:40, :] = packed
        cs[f, 7:8, :] = jnp.ones((1, 128), F32)
        cs[f, 40:41, :] = jnp.ones((1, 128), F32)

    middle = (lax.rem(l8, 32) >= 8) & (lax.rem(l8, 32) < 16)

    def gather_fields(items):
        total = None
        for j, item in items:
            shift = (8 * j - 8) % 128
            item = jnp.where(middle, item, 0.0)
            part = pltpu.roll(item, shift, 1) if shift else item
            total = part if total is None else total + part
        return total

    def of_line(groups, k):
        block = jnp.zeros((8, 128), F32)
        for g, group in groups.items():
            shift = (32 * g - 32 * k) % 128
            block = jnp.where(l8 // 32 == g, pltpu.roll(group, shift, 1) if shift else group, block)
        return block

    for yb in range(4):
        here = [cs[f, 8 + 8 * yb:16 + 8 * yb, :] for f in range(5)]
        above = [cs[f, 9 + 8 * yb:17 + 8 * yb, :] for f in range(5)]
        below = [cs[f, 7 + 8 * yb:15 + 8 * yb, :] for f in range(5)]
        w, c = state(here), sound(here)
        fz = face(side(here, w, c, 2), cell([pltpu.roll(a, 120, 1) for a in here], 2))
        centre = side(here, w, c, 1)
        fu, fd = face(centre, cell(above, 1)), face(cell(below, 1), centre)
        if yb == 0:
            fd = [jnp.where(s8 == 0, 0.0, a) for a in fd]
        if yb == 3:
            fu = [jnp.where(s8 == 7, 0.0, a) for a in fu]
        moved = [(fu[k] - fd[k]) + (fz[k] - pltpu.roll(fz[k], 8, 1)) for k in range(5)]
        items = list(here) + moved
        groups = {g: gather_fields(list(enumerate(items[4 * g:4 * g + 4]))) for g in range(3)}
        for k in range(4):
            xs[32 * k + 8 * yb:32 * k + 8 * yb + 8, :] = of_line(groups, k)

    def parts(a):
        hi = a.astype(jnp.bfloat16)
        rest = a - hi.astype(F32)
        mid = rest.astype(jnp.bfloat16)
        return hi, mid, (rest - mid.astype(F32)).astype(jnp.bfloat16)

    dot = functools.partial(jnp.dot, preferred_element_type=F32)
    hi, mid, lo = parts(xs[...])
    chosen = oh[...]
    base[...] = dot(chosen, hi) + (dot(chosen, mid) + dot(chosen, lo))

    for u in range(65):
        o = s8 + (8 * u - 8) - 8 * (l8 // 4)
        o = jnp.where(o >= NX // 2, o - NX, o)
        table[8 * u:8 * u + 8, :] = o.astype(F32)

    for c in near:
        c.wait_recv()
    first = s8 == 0
    left, right = [], []
    for f in range(5):
        wide8 = lambda a: jnp.broadcast_to(a, (8, 128))
        left.append(jnp.where(first, wide8(cr[0, f:f + 1, :]), wide8(cs[f, 39:40, :])))
        right.append(jnp.where(first, wide8(cs[f, 8:9, :]), wide8(cr[1, f:f + 1, :])))
    fe = [jnp.where(first, -a, a) for a in face(cell(left, 1), cell(right, 1))]
    groups = {1: gather_fields(list(enumerate(fe[:3], 1))), 2: gather_fields(list(enumerate(fe[3:])))}
    extra = parts(jnp.concatenate([of_line(groups, k) for k in range(4)], axis=0))
    blank = jnp.zeros((32, 128), jnp.bfloat16)
    added = dot(ohc[...], jnp.concatenate(list(extra) + [blank], axis=0))
    best = jnp.maximum(jnp.maximum(best, mr[...])[5:6, :], jnp.maximum(cr[0, 5:6, :], cr[1, 5:6, :]))
    sent = jnp.where(iota((NSLAB * MOST, 128), 1) >= 80, jnp.broadcast_to(best, (NSLAB * MOST, 128)), base[...] + added)
    ps[...] = sent.reshape(NSLAB, MOST, 128)

    def deliver(q):
        remote(ps.at[q], r_out.at[me], as_sem, ar_sem, {"slab": q}).start()

    @pl.when(me != HUB)
    def _():
        pl.semaphore_wait(go, 1)

    for a, b, c in PARTNERS:
        deliver(slab_of(a, b, lax.rem(row_z + c, 8)))
    mine = pltpu.make_async_copy(ps.at[me], r_out.at[me], loc_sem)
    mine.start()

    for c in sides:
        c.wait_recv()
    for f in range(5):
        U[f, 1:9, 7, :] = hr[0, f]
        U[f, 1:9, 40, :] = hr[1, f]

    def dense(x, carry):
        for yb in range(4):
            lo, hi = 8 + 8 * yb, 16 + 8 * yb
            here = [U[f, x + 1, lo:hi, :] for f in range(5)]
            w, c = state(here), sound(here)
            fz = face(side(here, w, c, 2), cell([pltpu.roll(a, 127, 1) for a in here], 2))
            moved = [fz[k] - pltpu.roll(fz[k], 1, 1) for k in range(5)]
            for d, pair in ((1, ((1, 1), (1, -1))), (0, ((2, 0), (0, 0)))):
                (xu, yu), (xd, yd) = pair
                mid = side(here, w, c, d)
                fu = face(mid, cell([U[f, x + xu, lo + yu:hi + yu, :] for f in range(5)], d))
                fd = face(cell([U[f, x + xd, lo + yd:hi + yd, :] for f in range(5)], d), mid)
                moved = [moved[k] + (fu[k] - fd[k]) for k in range(5)]
            for k in range(5):
                w_out[k, x, lo - 8:hi - 8, :] = w[k]
                d_out[k, x, lo - 8:hi - 8, :] = moved[k]
        return carry

    lax.fori_loop(1, NXL - 1, dense, 0)
    for c in ends:
        c.wait_recv()
    lax.fori_loop(0, 2, lambda i, carry: dense((NXL - 1) * i, carry), 0)

    mine.wait()
    for c in near + sides + ends:
        c.wait_send()
    most = pl.ds(0, NSLAB - 1)
    pltpu.make_async_copy(ps.at[most], ps.at[most], as_sem).wait()
    pltpu.make_async_copy(r_out.at[most], r_out.at[most], ar_sem).wait()


def final_kernel(w_ref, d_ref, r_ref, table, own_hbm, new_hbm, od, nb, pb, acc, own, sem, own_sem):
    me = lax.axis_index("slab").astype(F32)
    owned = pltpu.make_async_copy(own_hbm, own, own_sem)
    owned.start()
    arrived = r_ref[...]
    fastest = jnp.max(jnp.max(arrived, axis=0), axis=0, keepdims=True)[:, 96:97]
    half_dt = (0.5 * COURANT) / fastest
    hdt = jnp.broadcast_to(half_dt, (8, 128))

    outs = []
    for k in range(5):
        for x in range(NXL):
            for yb in range(4):
                at = (k, x, slice(8 * yb, 8 * yb + 8))
                nb[at] = w_ref[at] - hdt * d_ref[at]
        outs.append(pltpu.make_async_copy(nb.at[k], new_hbm.at[k], sem.at[k]))
        outs[-1].start()

    turned = jnp.transpose(arrived.reshape(NSLAB * MOST, 128))
    fields = [turned[8 * f:8 * f + 8, :] for f in range(10)]
    here, moved = fields[:5], fields[5:]
    s2 = iota((8, NSLAB * MOST), 0)

    def after(a):
        a = pltpu.roll(a, 7, 0)
        return jnp.where(s2 < 7, a, pltpu.roll(a, NSLAB * MOST - 4, 1))

    def before(a):
        a = pltpu.roll(a, 1, 0)
        return jnp.where(s2 > 0, a, pltpu.roll(a, 4, 1))

    w = state(here)
    fx = face(side(here, w, sound(here), 0), cell([after(a) for a in here], 0))
    hdt2 = jnp.broadcast_to(half_dt, (8, NSLAB * MOST))
    new = [w[k] - hdt2 * (moved[k] + (fx[k] - before(fx[k]))) for k in range(5)]
    r = new[0]
    v = [new[1 + k] / r for k in range(3)]
    p = (GAMMA - 1.0) * (new[4] - 0.5 * (new[1] * v[0] + new[2] * v[1] + new[3] * v[2]))
    broad = TURBULENT + p / r
    inverse = math.sqrt(LOG2E) / (8.0 * jnp.sqrt(broad))
    moved_by = (64.0 * v[0]) * inverse
    level = jnp.log2((NORMALISE / 8.0) * (r * r)) - 1.2 * jnp.log2(broad)
    for n, param in enumerate((inverse, moved_by, level)):
        for h in range(2):
            for x in range(8):
                pb[n, 8 * h + x] = jnp.broadcast_to(param[x:x + 1, 128 * h:128 * h + 128], (8, 128))

    def pixels(block, carry):
        first = pl.multiple_of(128 * block, 128)
        starts = (first, pl.multiple_of(lax.rem(first + NX // 2, NX), 128))
        sums = [None] * 16
        for h in range(2):
            for x in range(8):
                inv, mov, lev = (pb[n, 8 * h + x] for n in range(3))
                for j in range(16):
                    o = table[pl.ds(starts[h] + (8 * j + 8 - x), 8), :]
                    z = o * inv - mov
                    part = jnp.exp2(lev - z * z)
                    sums[j] = part if sums[j] is None else sums[j] + part
        for j in range(16):
            acc[pl.ds(first + 8 * j, 8), :] = sums[j]
        return carry

    lax.fori_loop(0, 4, pixels, 0)
    depth = jnp.transpose(acc[...])
    both = depth[0:8, :]
    for n in range(1, 16):
        both = both + depth[8 * n:8 * n + 8, :]
    owned.wait()
    row = jnp.concatenate([own[k].astype(F32) for k in range(4)], axis=1)
    held = jnp.sum(jnp.where(row == me, 1.0, 0.0), axis=1, keepdims=True)
    valid = iota((4, NX), 0).astype(F32) < held
    od[0, 0] = jnp.where(valid, both[0:4, :] + both[4:8, :], 0.0)
    for out in outs:
        out.wait()


def body(density, velocity, pressure, owners):
    own = jnp.transpose(owners, (1, 2, 0))
    density, velocity, pressure, own = (pltpu.with_memory_space_constraint(a, pltpu.HBM) for a in (density, velocity, pressure, own))
    vmem = pl.BlockSpec(memory_space=pltpu.VMEM)
    hbm = pl.BlockSpec(memory_space=pltpu.HBM)
    dense = jax.ShapeDtypeStruct((5, NXL, CY, NZ), F32)
    arrived = jax.ShapeDtypeStruct((NSLAB, MOST, 128), F32)
    offsets = jax.ShapeDtypeStruct((NX + 8, 128), F32)
    dma, regular = pltpu.SemaphoreType.DMA, pltpu.SemaphoreType.REGULAR
    w, d, r, table = pl.pallas_call(
        comm_kernel,
        out_shape=(dense, dense, arrived, offsets),
        in_specs=[hbm, hbm, hbm, hbm],
        out_specs=(vmem, vmem, vmem, vmem),
        scratch_shapes=[
            pltpu.VMEM((5, NXL + 2, CY + 16, NZ), F32),
            pltpu.VMEM((2, 5, 8, 128), F32),
            pltpu.VMEM((2, 5, 8, 128), F32),
            pltpu.VMEM((2, 8, 128), F32),
            pltpu.VMEM((2, 8, 128), F32),
            pltpu.VMEM((8, 128), F32),
            pltpu.VMEM((8, 128), F32),
            pltpu.VMEM((5, CY + 16, 128), F32),
            pltpu.VMEM((128, 128), F32),
            pltpu.VMEM((NSLAB * MOST, 128), jnp.bfloat16),
            pltpu.VMEM((NSLAB * MOST, 128), jnp.bfloat16),
            pltpu.VMEM((NSLAB * MOST, 128), F32),
            pltpu.VMEM((NSLAB, MOST, 128), F32),
            pltpu.VMEM((4, 1, CY), jnp.int32),
            dma((7,)), dma((5,)), dma((5,)), dma((2,)), dma((2,)), dma, dma, dma, regular,
        ],
        compiler_params=pltpu.CompilerParams(collective_id=0, has_side_effects=True, vmem_limit_bytes=24 << 20),
        name="exchange",
    )(density, velocity, pressure, own)
    return tuple(pl.pallas_call(
        final_kernel,
        out_shape=(dense, jax.ShapeDtypeStruct((1, 1, MOST, NX), F32)),
        in_specs=[vmem, vmem, vmem, vmem, hbm],
        out_specs=(hbm, vmem),
        scratch_shapes=[
            pltpu.VMEM((5, NXL, CY, NZ), F32),
            pltpu.VMEM((3, 16, 8, 128), F32),
            pltpu.VMEM((NX, 128), F32),
            pltpu.VMEM((4, 1, CY), jnp.int32),
            dma((5,)), dma,
        ],
        compiler_params=pltpu.CompilerParams(vmem_limit_bytes=24 << 20),
        name="finish",
    )(w, d, r, table, own))


def solution(mesh):
    placed = (P("slab", "sect", None), P(None, "slab", "sect", None), P("slab", "sect", None), P("sect", None, None))
    return jax.shard_map(body, mesh=mesh, in_specs=placed, out_specs=(P(None, "slab", "sect", None), P("sect", "slab", None, None)),
                         check_vma=False)
```

time: 25.1 us -> 23.4 us (0.932)
  Pallas kernels: 24.4 us -> 22.7 us
    pallas_call x1, Pallas kernels: 21.8 us -> 20.5 us  [body(): pl.pallas_call(comm_kernel, out_shape=(dense, dense, arrived, offsets), i...]
    pallas_call x1, Pallas kernels: 2.56 us -> 2.15 us  [body(): pl.pallas_call(final_kernel, out_shape=(dense, jax.ShapeDtypeStruct((1, 1...]
where the time goes in v4:
time: 23.4 us; the launch traced here: 23.3 us
  Pallas kernels  22.7 us (97%)
  between operations  0.64 us (3%)
    pallas_call x1, Pallas kernels, body(): pl.pallas_call(comm_kernel, out_shape=(dense, dense, arrived, offsets), i...  20.5 us
    pallas_call x1, Pallas kernels, body(): pl.pallas_call(final_kernel, out_shape=(dense, jax.ShapeDtypeStruct((1, 1...  2.15 us

profile of v4, /device:TPU:1, one launch (start us, length us, event | category | flops | bytes accessed | tf_op | source)
XLA Modules:
  0.0 23.3 jit_solution(10002132793021273305)
XLA Ops:
  0.6 20.5 %exchange.1 = (f32[5,8,32,128]{3,2,1,0:T(8,128)S(1)}, f32[5,8,32,128]{3,2,1,0:T(8,128)S(1)}, f32[64,4,128]{2,1,0:T(4,128)S(1)}, f32[520,128]{1,0:T(8,128)S(1)}) custom-call(f32[8,32,128]{2,1,0:T(8,128)} %den.1, f32[3,8,32,128]{3,2,1,0:T(8,128)} %vel.1, f32[8,32,128]{2,1,0:T(8,128)} %pre.1, s32[4,1,32]{2,1,0:T(1,128)} %bitcast.1), custom_call_target="tpu_custom_call" | custom-call | tf_op jit(solution)/shard_map/exchange/pallas_call | solution.py:397
  21.2 2.2 %finish.1 = (f32[5,8,32,128]{3,2,1,0:T(8,128)}, f32[1,1,4,512]{3,2,1,0:T(4,128)}) custom-call(f32[5,8,32,128]{3,2,1,0:T(8,128)S(1)} %get-tuple-element.6.w_ref, f32[5,8,32,128]{3,2,1,0:T(8,128)S(1)} %get-tuple-element.7.d_ref, f32[64,4,128]{2,1,0:T(4,128)S(1)} %get-tuple-element.8.r_ref, f32[520,128]{1,0:T(8,128)S(1)} %get-tuple-element.9.table, ...), custom_call_target="tpu_custom_call" | custom-call | tf_op jit(solution)/shard_map/finish/pallas_call | solution.py:422

commit v5 on v4

--- a/solution.py
+++ b/solution.py
@@ -102,12 +102,6 @@
     @pl.when(before != HUB)
     def _():
         tell(barrier, before)
-
-    @pl.when(me == HUB)
-    def _():
-        pl.semaphore_wait(barrier, NSLAB - 1 + NSECT - 1)
-        for q in FROM_HUB:
-            tell(go, q)
 
     best = jnp.zeros((8, 128), F32)
     for half in range(2):
@@ -135,6 +129,11 @@
     def _():
         pl.semaphore_wait(barrier, NSECT + 1)
 
+    @pl.when(me == HUB)
+    def _():
+        pl.semaphore_wait(barrier, NSLAB - 1 + NSECT - 1)
+
+
     def remote(src, dst, ssem, rsem, where):
         return pltpu.make_async_remote_copy(src_ref=src, dst_ref=dst, send_sem=ssem, recv_sem=rsem, device_id=where,
                                             device_id_type=MESH)
@@ -155,6 +154,11 @@
     ]
     for c in near + sides + ends:
         c.start()
+
+    @pl.when(me == HUB)
+    def _():
+        for q in FROM_HUB:
+            tell(go, q)
 
     owned.wait()
     row = jnp.concatenate([own[k].astype(F32) for k in range(4)], axis=1)

time: 23.4 us -> 22.9 us (0.979)
  Pallas kernels: 22.7 us -> 22.1 us
    pallas_call x1, Pallas kernels: 20.5 us -> 20 us  [body(): pl.pallas_call(comm_kernel, out_shape=(dense, dense, arrived, offsets), i...]
where the time goes in v5:
time: 22.9 us; the launch traced here: 22.8 us
  Pallas kernels  22.1 us (97%)
  between operations  0.64 us (3%)
    pallas_call x1, Pallas kernels, body(): pl.pallas_call(comm_kernel, out_shape=(dense, dense, arrived, offsets), i...  20 us
    pallas_call x1, Pallas kernels, body(): pl.pallas_call(final_kernel, out_shape=(dense, jax.ShapeDtypeStruct((1, 1...  2.15 us

profile of v5, /device:TPU:1, one launch (start us, length us, event | category | flops | bytes accessed | tf_op | source)
XLA Modules:
  0.0 22.8 jit_solution(1706303985518940360)
XLA Ops:
  0.6 20.0 %exchange.1 = (f32[5,8,32,128]{3,2,1,0:T(8,128)S(1)}, f32[5,8,32,128]{3,2,1,0:T(8,128)S(1)}, f32[64,4,128]{2,1,0:T(4,128)S(1)}, f32[520,128]{1,0:T(8,128)S(1)}) custom-call(f32[8,32,128]{2,1,0:T(8,128)} %den.1, f32[3,8,32,128]{3,2,1,0:T(8,128)} %vel.1, f32[8,32,128]{2,1,0:T(8,128)} %pre.1, s32[4,1,32]{2,1,0:T(1,128)} %bitcast.1), custom_call_target="tpu_custom_call" | custom-call | tf_op jit(solution)/shard_map/exchange/pallas_call | solution.py:401
  20.6 2.2 %finish.1 = (f32[5,8,32,128]{3,2,1,0:T(8,128)}, f32[1,1,4,512]{3,2,1,0:T(4,128)}) custom-call(f32[5,8,32,128]{3,2,1,0:T(8,128)S(1)} %get-tuple-element.6.w_ref, f32[5,8,32,128]{3,2,1,0:T(8,128)S(1)} %get-tuple-element.7.d_ref, f32[64,4,128]{2,1,0:T(4,128)S(1)} %get-tuple-element.8.r_ref, f32[520,128]{1,0:T(8,128)S(1)} %get-tuple-element.9.table, ...), custom_call_target="tpu_custom_call" | custom-call | tf_op jit(solution)/shard_map/finish/pallas_call | solution.py:426

commit v6 on v5

--- a/solution.py
+++ b/solution.py
@@ -23,7 +23,7 @@
 F32 = jnp.float32
 LOG2E = math.log2(math.e)
 HOPS = lambda a, b, c: 2 * a + min(b, 4 - b) + min(c, 8 - c)
-PARTNERS = sorted(((a, b, c) for a in range(2) for b in range(4) for c in range(8) if a + b + c), key=lambda o: -HOPS(*o))
+FROM_ORIGIN = sorted(range(NSLAB), key=lambda q: HOPS(q // 32, q // 8 % 4, min(q % 8, 4)))
 HUB = 53
 FROM_HUB = sorted((q for q in range(NSLAB) if q != HUB),
                   key=lambda q: HOPS((q // 32 - 1) % 2, (q // 8 % 4 - 2) % 4, (q % 8 - 5) % 8))
@@ -65,7 +65,6 @@
                 hr_sem, xs_sem, xr_sem, loc_sem, as_sem, ar_sem, go):
     me = lax.axis_index("slab")
     sect = lax.axis_index("sect")
-    far, row_y, row_z = me // 32, lax.rem(me // 8, 4), lax.rem(me, 8)
     owned = pltpu.make_async_copy(own_hbm, own, in_sem.at[6])
     copies = []
     for half in range(2):
@@ -75,16 +74,13 @@
             pltpu.make_async_copy(vel.at[:, some], U.at[(pl.ds(1, 3),) + to], in_sem.at[3 * half + 1]),
             pltpu.make_async_copy(pre.at[some], U.at[(4,) + to], in_sem.at[3 * half + 2]),
         ]
+    barrier = pltpu.get_barrier_semaphore()
+    for i in range(1, NSECT):
+        pl.semaphore_signal(barrier, inc=1, device_id={"sect": lax.rem(sect + i, NSECT)}, device_id_type=MESH)
+
     for c in copies:
         c.start()
     owned.start()
-
-    def slab_of(step_x, step_y, z):
-        return lax.rem(far + step_x, 2) * 32 + lax.rem(row_y + step_y, 4) * 8 + z
-
-    barrier = pltpu.get_barrier_semaphore()
-    for i in range(1, NSECT):
-        pl.semaphore_signal(barrier, inc=1, device_id={"sect": lax.rem(sect + i, NSECT)}, device_id_type=MESH)
 
     def tell(sem, q):
         pl.semaphore_signal(sem, inc=1, device_id={"slab": q}, device_id_type=MESH)
@@ -122,7 +118,9 @@
             turned = pltpu.roll(edge, 8, 1, stride=1, stride_axis=0)
             cm[way, f:f + 1, :] = jnp.sum(jnp.where(pick, turned, 0.0), axis=0, keepdims=True)
     for way in range(2):
-        cm[way, 5:8, :] = best[5:8, :]
+        cm[way, 5:6, :] = best[5:6, :]
+        cm[way, 6:7, :] = sound([cm[way, f:f + 1, :] for f in range(5)])
+        cm[way, 7:8, :] = best[7:8, :]
     ms[...] = best
 
     @pl.when(me != HUB)
@@ -246,17 +244,26 @@
         o = jnp.where(o >= NX // 2, o - NX, o)
         table[8 * u:8 * u + 8, :] = o.astype(F32)
 
+    first = s8 == 0
+    sign = jnp.where(first, -1.0, 1.0)
+    wide8 = lambda low, high: jnp.where(first, jnp.broadcast_to(low, (8, 128)), jnp.broadcast_to(high, (8, 128)))
+    wk, fk, ak = cell([wide8(cs[f, 8:9, :], cs[f, 39:40, :]) for f in range(5)], 1)
     for c in near:
         c.wait_recv()
-    first = s8 == 0
-    left, right = [], []
-    for f in range(5):
-        wide8 = lambda a: jnp.broadcast_to(a, (8, 128))
-        left.append(jnp.where(first, wide8(cr[0, f:f + 1, :]), wide8(cs[f, 39:40, :])))
-        right.append(jnp.where(first, wide8(cs[f, 8:9, :]), wide8(cr[1, f:f + 1, :])))
-    fe = [jnp.where(first, -a, a) for a in face(cell(left, 1), cell(right, 1))]
-    groups = {1: gather_fields(list(enumerate(fe[:3], 1))), 2: gather_fields(list(enumerate(fe[3:])))}
-    extra = parts(jnp.concatenate([of_line(groups, k) for k in range(4)], axis=0))
+    beyond = [wide8(cr[0, f:f + 1, :], cr[1, f:f + 1, :]) for f in range(7)]
+    wb, fb, ab = side(beyond[:5], state(beyond[:5]), beyond[6], 1)
+    speed = jnp.maximum(ak, ab)
+    fe = [jnp.where(middle, sign * (fk[k] + fb[k]) + speed * (wk[k] - wb[k]), 0.0) for k in range(5)]
+
+    def edge_lines(k):
+        total = None
+        for f in range(5):
+            shift = (8 * (5 + f) - 8 - 32 * k) % 128
+            part = jnp.where(l8 // 8 == 5 + f, pltpu.roll(fe[f], shift, 1) if shift else fe[f], 0.0)
+            total = part if total is None else total + part
+        return total
+
+    extra = parts(jnp.concatenate([edge_lines(k) for k in range(4)], axis=0))
     blank = jnp.zeros((32, 128), jnp.bfloat16)
     added = dot(ohc[...], jnp.concatenate(list(extra) + [blank], axis=0))
     best = jnp.maximum(jnp.maximum(best, mr[...])[5:6, :], jnp.maximum(cr[0, 5:6, :], cr[1, 5:6, :]))
@@ -270,8 +277,8 @@
     def _():
         pl.semaphore_wait(go, 1)
 
-    for a, b, c in PARTNERS:
-        deliver(slab_of(a, b, lax.rem(row_z + c, 8)))
+    for q in FROM_ORIGIN:
+        pl.when(q != me)(functools.partial(deliver, q))
     mine = pltpu.make_async_copy(ps.at[me], r_out.at[me], loc_sem)
     mine.start()
 

time: 22.9 us -> 22.7 us (level)
  no operation moved by 1% of the time
where the time goes in v6:
time: 22.7 us; the launch traced here: 22.6 us
  Pallas kernels  22 us (97%)
  between operations  0.64 us (3%)
    pallas_call x1, Pallas kernels, body(): pl.pallas_call(comm_kernel, out_shape=(dense, dense, arrived, offsets), i...  19.8 us
    pallas_call x1, Pallas kernels, body(): pl.pallas_call(final_kernel, out_shape=(dense, jax.ShapeDtypeStruct((1, 1...  2.15 us

profile of v6, /device:TPU:1, one launch (start us, length us, event | category | flops | bytes accessed | tf_op | source)
XLA Modules:
  0.0 22.6 jit_solution(386803505406815133)
XLA Ops:
  0.6 19.8 %exchange.1 = (f32[5,8,32,128]{3,2,1,0:T(8,128)S(1)}, f32[5,8,32,128]{3,2,1,0:T(8,128)S(1)}, f32[64,4,128]{2,1,0:T(4,128)S(1)}, f32[520,128]{1,0:T(8,128)S(1)}) custom-call(f32[8,32,128]{2,1,0:T(8,128)} %den.1, f32[3,8,32,128]{3,2,1,0:T(8,128)} %vel.1, f32[8,32,128]{2,1,0:T(8,128)} %pre.1, s32[4,1,32]{2,1,0:T(1,128)} %bitcast.1), custom_call_target="tpu_custom_call" | custom-call | tf_op jit(solution)/shard_map/exchange/pallas_call | solution.py:408
  20.5 2.2 %finish.1 = (f32[5,8,32,128]{3,2,1,0:T(8,128)}, f32[1,1,4,512]{3,2,1,0:T(4,128)}) custom-call(f32[5,8,32,128]{3,2,1,0:T(8,128)S(1)} %get-tuple-element.6.w_ref, f32[5,8,32,128]{3,2,1,0:T(8,128)S(1)} %get-tuple-element.7.d_ref, f32[64,4,128]{2,1,0:T(4,128)S(1)} %get-tuple-element.8.r_ref, f32[520,128]{1,0:T(8,128)S(1)} %get-tuple-element.9.table, ...), custom_call_target="tpu_custom_call" | custom-call | tf_op jit(solution)/shard_map/finish/pallas_call | solution.py:433

commit v7 on v6

--- a/solution.py
+++ b/solution.py
@@ -367,22 +367,22 @@
                 pb[n, 8 * h + x] = jnp.broadcast_to(param[x:x + 1, 128 * h:128 * h + 128], (8, 128))
 
     def pixels(block, carry):
-        first = pl.multiple_of(128 * block, 128)
-        starts = (first, pl.multiple_of(lax.rem(first + NX // 2, NX), 128))
-        sums = [None] * 16
+        first = pl.multiple_of(256 * block, 256)
+        starts = (first, pl.multiple_of(lax.rem(first + NX // 2, NX), 256))
+        sums = [None] * 32
         for h in range(2):
             for x in range(8):
                 inv, mov, lev = (pb[n, 8 * h + x] for n in range(3))
-                for j in range(16):
+                for j in range(32):
                     o = table[pl.ds(starts[h] + (8 * j + 8 - x), 8), :]
                     z = o * inv - mov
                     part = jnp.exp2(lev - z * z)
                     sums[j] = part if sums[j] is None else sums[j] + part
-        for j in range(16):
+        for j in range(32):
             acc[pl.ds(first + 8 * j, 8), :] = sums[j]
         return carry
 
-    lax.fori_loop(0, 4, pixels, 0)
+    lax.fori_loop(0, 2, pixels, 0)
     depth = jnp.transpose(acc[...])
     both = depth[0:8, :]
     for n in range(1, 16):

time: 22.7 us -> 22.7 us (level)
  no operation moved by 1% of the time
where the time goes in v7:
time: 22.7 us; the launch traced here: 22.6 us
  Pallas kernels  22 us (97%)
  between operations  0.64 us (3%)
    pallas_call x1, Pallas kernels, body(): pl.pallas_call(comm_kernel, out_shape=(dense, dense, arrived, offsets), i...  19.8 us
    pallas_call x1, Pallas kernels, body(): pl.pallas_call(final_kernel, out_shape=(dense, jax.ShapeDtypeStruct((1, 1...  2.12 us

profile of v7, /device:TPU:1, one launch (start us, length us, event | category | flops | bytes accessed | tf_op | source)
XLA Modules:
  0.0 22.6 jit_solution(17588120192490134013)
XLA Ops:
  0.6 19.8 %exchange.1 = (f32[5,8,32,128]{3,2,1,0:T(8,128)S(1)}, f32[5,8,32,128]{3,2,1,0:T(8,128)S(1)}, f32[64,4,128]{2,1,0:T(4,128)S(1)}, f32[520,128]{1,0:T(8,128)S(1)}) custom-call(f32[8,32,128]{2,1,0:T(8,128)} %den.1, f32[3,8,32,128]{3,2,1,0:T(8,128)} %vel.1, f32[8,32,128]{2,1,0:T(8,128)} %pre.1, s32[4,1,32]{2,1,0:T(1,128)} %bitcast.1), custom_call_target="tpu_custom_call" | custom-call | tf_op jit(solution)/shard_map/exchange/pallas_call | solution.py:408
  20.5 2.1 %finish.1 = (f32[5,8,32,128]{3,2,1,0:T(8,128)}, f32[1,1,4,512]{3,2,1,0:T(4,128)}) custom-call(f32[5,8,32,128]{3,2,1,0:T(8,128)S(1)} %get-tuple-element.6.w_ref, f32[5,8,32,128]{3,2,1,0:T(8,128)S(1)} %get-tuple-element.7.d_ref, f32[64,4,128]{2,1,0:T(4,128)S(1)} %get-tuple-element.8.r_ref, f32[520,128]{1,0:T(8,128)S(1)} %get-tuple-element.9.table, ...), custom_call_target="tpu_custom_call" | custom-call | tf_op jit(solution)/shard_map/finish/pallas_call | solution.py:433
